TPU v7x, 32 devices: a whole 2x2x4 slice. The times are simulated.
32 devices in a mesh: section: 8 (over z, core), tensor: 2 (over x), replica: 2 (over y).
Axes of the slice: x: 2, y: 2, z: 4, core: 2. Of those that a mesh axis runs over, the one named last changes fastest.
Arguments:
- pool_inputs: bfloat16 [8, 256, 2, 1408], P('section', 'replica', None, 'tensor'), may hold values from -6 to 6
- pool_mixed: bfloat16 [8, 256, 1408], P('section', 'replica'), may hold values from -6 to 6
- crop_ids: int32 [8, 8, 128], P('section', 'replica'), may hold values from 0 to 127
- incoming: bfloat16 [8, 256, 1408], P('section', 'replica', 'tensor'), may hold values from -6 to 6
- loss_grads: bfloat16 [3, 256, 1408], P(None, 'replica', 'tensor'), may hold values from -6 to 6
- w_proj: bfloat16 [8, 2, 1408, 1408], P('section', None, ('tensor', 'replica')), may hold values from -0.109375 to 0.109375
- w_up: bfloat16 [8, 1408, 3072], P('section', None, ('tensor', 'replica')), may hold values from -0.15625 to 0.15625
- w_down: bfloat16 [8, 3072, 1408], P('section', ('tensor', 'replica')), may hold values from -0.109375 to 0.109375
Outputs:
- grad_proj: bfloat16 [8, 2, 1408, 1408], P('section', None, ('tensor', 'replica'))
- grad_up: bfloat16 [8, 1408, 3072], P('section', None, ('tensor', 'replica'))
- grad_down: bfloat16 [8, 3072, 1408], P('section', ('tensor', 'replica'))
- outgoing: bfloat16 [8, 256, 2, 1408], P('section', 'replica', None, 'tensor')
All inputs are finite; a program needn't handle non-finite values.
Results may differ from a plain program's by a relative error of at most 0.02.
Values may be sent and summed in bfloat16 or wider, within the bound.
A program may use at most 128 MiB of HBM per device.

v0:
```python
import functools

import jax
import jax.numpy as jnp
from jax import lax
from jax.experimental import pallas as pl
from jax.experimental.pallas import tpu as pltpu
from jax.sharding import PartitionSpec as P

gelu_scale = 0.7978845608
gelu_cubic = 0.044715
bf16, f32 = jnp.bfloat16, jnp.float32
MESH = pl.DeviceIdType.MESH


def gelu_pair(pre_gelu):
    inner = gelu_scale * (pre_gelu + gelu_cubic * pre_gelu * pre_gelu * pre_gelu)
    tanh_part = jnp.tanh(inner)
    gelu_value = 0.5 * pre_gelu * (1.0 + tanh_part)
    gelu_slope = 0.5 * (1.0 + tanh_part) + 0.5 * pre_gelu * (
        1.0 - tanh_part * tanh_part
    ) * gelu_scale * (1.0 + 3.0 * gelu_cubic * pre_gelu * pre_gelu)
    return (gelu_value, gelu_slope)


def dot(a, b):
    return jnp.dot(a, b, preferred_element_type=f32)


def dot_nt(a, b):
    return lax.dot_general(a, b, (((1,), (1,)), ((), ())), preferred_element_type=f32)


def ticks_kernel(
    sections, tensors, replicas, own, ticks,
    inputs_hbm, pool_hbm, ids_hbm, seed_hbm, loss_hbm, proj_hbm, up_hbm, down_hbm,
    inputs_t, pool, act_t, sum_hidden, sum_grad, sum_up, out_t,
    proj, up, down, in_src, pool_src, ids_src, seed_src, loss_src, ids, loss_t,
    upstream, grads, hidden, part, got, own_part, slope_hi, slope_lo, slope, edge, edge_got,
    acc_hidden, acc_grad, acc_up,
    load_sem, place_sem, pool_sems, inputs_sems, ids_sems, loss_sems, seed_sems,
    part_sems, grad_sems, up_sems, edge_sems, out_sems,
):
    members = tensors * replicas
    section = lax.axis_index("section")
    tensor = lax.axis_index("tensor")
    replica = lax.axis_index("replica")
    me = tensor * replicas + replica
    hidden_rows = down.shape[0]

    def device(s, member):
        return {
            "section": s,
            "tensor": lax.div(member, replicas),
            "replica": lax.rem(member, replicas),
        }

    def member_at(by):
        return lax.rem(me + by, members)

    def replica_at(by):
        return lax.rem(replica + by, replicas)

    def load(i, src, dst):
        copy = pltpu.make_async_copy(src, dst, load_sem.at[i])
        copy.start()
        return copy

    pairs = [
        (pool_hbm, pool_src), (seed_hbm, seed_src), (ids_hbm, ids_src), (inputs_hbm, in_src),
        (loss_hbm, loss_src), (up_hbm, up), (down_hbm, down), (proj_hbm, proj),
    ]
    loads = [load(i, src, dst) for i, (src, dst) in enumerate(pairs)]
    ld_pool, ld_seed, ld_ids, ld_in, ld_loss, ld_up, ld_down, ld_proj = loads

    barrier = pltpu.get_barrier_semaphore()
    above = lax.rem(section + 1, sections)
    below = lax.rem(section + sections - 1, sections)
    mirror = sections - 1 - section
    for by in range(1, members):
        pl.semaphore_signal(barrier, 1, device_id=device(section, member_at(by)), device_id_type=MESH)
    for other in (above, below, mirror):
        pl.semaphore_signal(barrier, 1, device_id=device(other, me), device_id_type=MESH)
    pl.semaphore_wait(barrier, members - 1 + 3)

    sent = []

    def send(src, dst, sems, index, target):
        copy = pltpu.make_async_remote_copy(
            src_ref=src, dst_ref=dst, send_sem=sems.at[(0,) + index], recv_sem=sems.at[(1,) + index],
            device_id=target, device_id_type=MESH,
        )
        copy.start()
        sent.append(copy)
        return copy

    def over_replicas(src_of, dst, sems):
        return [
            send(src_of(replica_at(by)), dst, sems, (by - 1,),
                 device(section, tensor * replicas + replica_at(by)))
            for by in range(1, replicas)
        ]

    def place(i, src, dst):
        copy = pltpu.make_async_copy(src, dst, place_sem.at[i])
        copy.start()
        return copy

    slab = pl.ds(pl.multiple_of(me * own, 16), own)
    wide = pl.ds(pl.multiple_of(tensor * (replicas * own), 16), replicas * own)
    ld_pool.wait()
    pool_in = over_replicas(lambda r: pool_src, pool.at[replica], pool_sems)
    places = [place(0, pool_src, pool.at[replica])]
    ld_ids.wait()
    ids_in = over_replicas(lambda r: ids_src, ids.at[replica], ids_sems)
    ld_seed.wait()
    seed_to = upstream.at[0, replica, wide]
    seed_in = [
        send(seed_src, seed_to, seed_sems, (by - 1,), device(section, member_at(by)))
        for by in range(1, members)
    ]
    places.append(place(1, seed_src, seed_to))
    places.append(place(2, ids_src, ids.at[replica]))
    ld_in.wait()
    places.append(place(3, in_src.at[replica], inputs_t.at[replica]))
    ld_loss.wait()
    places.append(place(4, loss_src.at[replica], loss_t.at[replica]))
    is_top = section == sections - 1
    loss_in = []
    for by in range(1, replicas):
        to = replica_at(by)
        loss_in.append(pltpu.make_async_remote_copy(
            src_ref=loss_src.at[to], dst_ref=loss_t.at[replica],
            send_sem=loss_sems.at[0, by - 1], recv_sem=loss_sems.at[1, by - 1],
            device_id=device(section, tensor * replicas + to), device_id_type=MESH,
        ))

    acc_hidden[...] = jnp.zeros_like(acc_hidden)
    acc_grad[...] = jnp.zeros_like(acc_grad)
    acc_up[...] = jnp.zeros_like(acc_up)

    ld_up.wait()
    places[0].wait()
    step = 128

    for by in range(replicas):
        r = lax.rem(replica + replicas - by, replicas)
        if by > 0:
            pool_in[by - 1].wait_recv()

        def pre_at(cols, r=r):
            value, gelu_slope = gelu_pair(dot(pool[r], up[:, cols]).T)
            act_t[r, cols, :] = value.astype(bf16)
            high = gelu_slope.astype(bf16)
            slope_hi[r, cols, :] = high
            slope_lo[r, cols, :] = (gelu_slope - high.astype(f32)).astype(bf16)

        @pl.loop(0, hidden_rows // step)
        def _(c):
            pre_at(pl.ds(pl.multiple_of(c * step, step), step))

        if hidden_rows % step:
            pre_at(pl.ds(hidden_rows - hidden_rows % step, hidden_rows % step))

    places[2].wait()
    for copy in ids_in:
        copy.wait_recv()

    def picks(t, r):
        row = ids[r, pl.ds(t, 1), :]
        place_of = lax.broadcasted_iota(jnp.int32, (pool.shape[1], row.shape[1]), 0)
        return jnp.where(place_of == row, 1.0, 0.0).astype(bf16)

    def pick_slope(t, r):
        chosen = picks(t, r)
        slope[r] = dot(slope_hi[r], chosen) + dot(slope_lo[r], chosen)

    for r in range(replicas):
        pick_slope(0, r)

    ld_down.wait()
    ld_proj.wait()
    places[1].wait()
    for copy in seed_in:
        copy.wait_recv()

    up_in = {}
    part_in, grad_in, edge_in = {}, {}, {}

    def stage_hidden(t, r):
        for copy in up_in.get((t, r), ()):
            copy.wait_recv()
        hidden[t, r] = (dot(down[...], upstream[t, r]) * slope[r]).astype(bf16)
        copies = []
        for by in range(1, members):
            to = member_at(by)
            rows = pl.ds(pl.multiple_of(to * own, 16), own)
            part[t, r, by - 1] = dot(up[rows, :], hidden[t, r]).astype(bf16)
            copies.append(send(part.at[t, r, by - 1], got.at[t, r, by - 1], part_sems,
                               (t, r, by - 1), device(section, to)))
        own_part[r] = dot(up[slab, :], hidden[t, r]) + upstream[t, r, slab, :].astype(f32)
        part_in[t, r] = copies

    def stage_sum(t, r):
        total = own_part[r]
        for by in range(1, members):
            part_in[t, r][by - 1].wait_recv()
            total = total + got[t, r, by - 1].astype(f32)
        grads[t, r, slab, :] = total.astype(bf16)
        mine = grads.at[t, r, slab]
        grad_in[t, r] = [
            send(mine, mine, grad_sems, (t, r, by - 1), device(section, member_at(by)))
            for by in range(1, members)
        ]

    def stage_project(t, r):
        for copy in grad_in[t, r]:
            copy.wait_recv()
        edge[t, r, 1] = dot(proj[1], grads[t, r]).astype(bf16)
        last = t + 1 == ticks
        if not last:
            skip = pltpu.make_async_remote_copy(
                src_ref=edge.at[t, r, 1], dst_ref=edge_got.at[t, r, 1],
                send_sem=edge_sems.at[0, t, r, 1], recv_sem=edge_sems.at[1, t, r, 1],
                device_id=device(mirror, me), device_id_type=MESH,
            )
            pl.when(section >= sections // 2)(skip.start)
        edge[t, r, 0] = dot(proj[0], grads[t, r]).astype(bf16)
        if not last:
            down_copy = pltpu.make_async_remote_copy(
                src_ref=edge.at[t, r, 0], dst_ref=edge_got.at[t, r, 0],
                send_sem=edge_sems.at[0, t, r, 0], recv_sem=edge_sems.at[1, t, r, 0],
                device_id=device(below, me), device_id_type=MESH,
            )
            pl.when(section > 0)(down_copy.start)
            edge_in[t, r] = (down_copy, skip)

    def stage_next(t, r):
        down_copy, skip = edge_in[t, r]

        @pl.when(section < sections // 2)
        def _():
            down_copy.wait_recv()
            skip.wait_recv()
            summed = edge_got[t, r, 0].astype(f32) + edge_got[t, r, 1].astype(f32)
            upstream[t + 1, r, slab, :] = summed.astype(bf16)

        @pl.when((section >= sections // 2) & (section < sections - 1))
        def _():
            down_copy.wait_recv()
            upstream[t + 1, r, slab, :] = edge_got[t, r, 0]

        @pl.when(section == sections - 1)
        def _():
            upstream[t + 1, r, slab, :] = loss_t[r, t]

        mine = upstream.at[t + 1, r, slab]
        up_in[t + 1, r] = [
            send(mine, mine, up_sems, (t, r, by - 1), device(section, member_at(by)))
            for by in range(1, members)
        ]

    every = range(replicas)
    for t in range(ticks):
        for r in every:
            stage_hidden(t, r)
        if t == 0:
            for copy in loss_in:
                pl.when(is_top)(copy.start)
        for r in every:
            stage_sum(t, r)
        for r in every:
            chosen = picks(t, r)
            acc_hidden[r] += dot_nt(chosen, hidden[t, r])
            acc_up[r] += dot_nt(chosen, upstream[t, r])
        if t + 1 < ticks:
            for r in every:
                pick_slope(t + 1, r)
        if t == 0:
            places[4].wait()
            for copy in loss_in:
                pl.when(is_top)(copy.wait_recv)
        for r in every:
            stage_project(t, r)
        if t == min(1, ticks - 1):
            inputs_in = over_replicas(lambda r: in_src.at[r], inputs_t.at[replica], inputs_sems)
        for r in every:
            if t + 1 < ticks:
                stage_next(t, r)
        for r in every:
            acc_grad[r] += dot_nt(picks(t, r), grads[t, r])

    last = ticks - 1
    outs = []
    for by in range(1, replicas):
        to = replica_at(by)
        outs.append(send(edge.at[last, to], out_t.at[replica], out_sems, (by - 1,),
                         device(section, tensor * replicas + to)))
    out_place = place(5, edge.at[last, replica], out_t.at[replica])
    sum_hidden[...] = acc_hidden[...].astype(bf16)
    sum_grad[...] = acc_grad[...].astype(bf16)
    sum_up[...] = acc_up[...].astype(bf16)
    for copy in outs + inputs_in:
        copy.wait_recv()
    out_place.wait()
    places[3].wait()
    for copy in loss_in:
        pl.when(is_top)(copy.wait_send)
    for copy in sent:
        copy.wait_send()
    for key in edge_in:
        down_copy, skip = edge_in[key]
        pl.when(section > 0)(down_copy.wait_send)
        pl.when(section >= sections // 2)(skip.wait_send)


def tail_kernel(
    replicas, keep_ref, act_hbm, sum_up_hbm, inputs_hbm, sum_grad_hbm, pool_hbm, sum_hidden_hbm,
    down_out, up_out, proj_out,
    act_t, sum_up, inputs_t, sum_grad, pool, sum_hidden, down_v, up_v, proj_v, load_sems, sems,
):
    copies = []
    pairs = [
        (act_hbm, act_t), (sum_up_hbm, sum_up), (inputs_hbm, inputs_t),
        (sum_grad_hbm, sum_grad), (pool_hbm, pool), (sum_hidden_hbm, sum_hidden),
    ]
    loads = [
        pltpu.make_async_copy(src, dst, load_sems.at[i]) for i, (src, dst) in enumerate(pairs)
    ]
    for copy in loads:
        copy.start()

    def finish(term, rows, kept, out, scale=None):
        total = 0.0
        for r in range(replicas):
            total = total + term(r).astype(bf16).astype(f32)
        if scale is not None:
            total = total * scale
        kept.at[rows][...] = total.astype(bf16)
        copy = pltpu.make_async_copy(kept.at[rows], out.at[rows], sems.at[len(copies)])
        copy.start()
        copies.append(copy)

    loads[0].wait()
    loads[1].wait()
    for start in range(0, down_v.shape[0], 128):
        rows = pl.ds(start, min(128, down_v.shape[0] - start))
        finish(lambda r: dot(act_t[r, rows, :], sum_up[r]), rows, down_v, down_out)
    loads[2].wait()
    loads[3].wait()
    half = proj_v.shape[1] // 2
    for k in range(2):
        for start in (0, half):
            rows = (k, pl.ds(start, half))
            finish(lambda r: dot(inputs_t[r, k, pl.ds(start, half), :], sum_grad[r]), rows,
                   proj_v, proj_out, keep_ref[0] if k else None)
    loads[4].wait()
    loads[5].wait()
    for start in range(0, up_v.shape[0], 128):
        rows = pl.ds(start, min(128, up_v.shape[0] - start))
        finish(lambda r: dot(pool[r, :, rows].T, sum_hidden[r]), rows, up_v, up_out)
    for copy in copies:
        copy.wait()


def body(pool_inputs, pool_mixed, crop_ids, incoming, loss_grads, w_proj, w_up, w_down):
    sections = lax.axis_size("section")
    tensors, replicas = lax.axis_size("tensor"), lax.axis_size("replica")
    members = tensors * replicas
    encoder = lax.axis_index("section") < sections // 2
    own = w_proj.shape[2]
    own_p = -(-own // 16) * 16
    rows, width = incoming.shape[1], w_up.shape[1]
    width_p = members * own_p
    hidden = w_up.shape[2]
    ticks = crop_ids.shape[1]
    saved = pool_mixed.shape[1]

    def padded(x, axis):
        if own == own_p:
            return x
        count = x.shape[axis] // own
        shape = x.shape[:axis] + (count, own) + x.shape[axis + 1:]
        fill = [(0, 0)] * (x.ndim + 1)
        fill[axis + 1] = (0, own_p - own)
        shape_p = x.shape[:axis] + (count * own_p,) + x.shape[axis + 1:]
        return jnp.pad(x.reshape(shape), fill).reshape(shape_p)

    proj = padded(padded(w_proj[0], 1), 2)
    up, down = padded(w_up[0], 0), padded(w_down[0], 1)
    pool_own = padded(pool_mixed[0], 1)
    keep = jnp.where(encoder, 0.0, 1.0).astype(f32)[None]
    features = pool_inputs[0].transpose(1, 2, 0)
    features = features.reshape(2, replicas, own, saved).transpose(1, 0, 2, 3)
    features = padded(features, 2)
    seed = padded(incoming[0].T, 0)
    loss = loss_grads.transpose(0, 2, 1).reshape(ticks - 1, replicas, own, rows)
    loss = padded(loss.transpose(1, 0, 2, 3), 2)

    shape = jax.ShapeDtypeStruct
    vmem = pl.BlockSpec(memory_space=pltpu.VMEM)
    hbm = pl.BlockSpec(memory_space=pl.ANY)
    dma = pltpu.SemaphoreType.DMA
    scratch = [
        pltpu.VMEM(proj.shape, bf16), pltpu.VMEM(up.shape, bf16), pltpu.VMEM(down.shape, bf16),
        pltpu.VMEM(features.shape, bf16), pltpu.VMEM(pool_own.shape, bf16),
        pltpu.VMEM(crop_ids.shape[1:], jnp.int32), pltpu.VMEM(seed.shape, bf16),
        pltpu.VMEM(loss.shape, bf16), pltpu.VMEM((replicas,) + crop_ids.shape[1:], jnp.int32),
        pltpu.VMEM((replicas, ticks - 1, own_p, rows), bf16),
        pltpu.VMEM((ticks, replicas, width_p, rows), bf16),
        pltpu.VMEM((ticks, replicas, width_p, rows), bf16),
        pltpu.VMEM((ticks, replicas, hidden, rows), bf16),
        pltpu.VMEM((ticks, replicas, members - 1, own_p, rows), bf16),
        pltpu.VMEM((ticks, replicas, members - 1, own_p, rows), bf16),
        pltpu.VMEM((replicas, own_p, rows), f32),
        pltpu.VMEM((replicas, hidden, saved), bf16), pltpu.VMEM((replicas, hidden, saved), bf16),
        pltpu.VMEM((replicas, hidden, rows), f32),
        pltpu.VMEM((ticks, replicas, 2, own_p, rows), bf16),
        pltpu.VMEM((ticks - 1, replicas, 2, own_p, rows), bf16),
        pltpu.VMEM((replicas, saved, hidden), f32), pltpu.VMEM((replicas, saved, width_p), f32),
        pltpu.VMEM((replicas, saved, width_p), f32),
        dma((8,)), dma((6,)), dma((2, replicas - 1)), dma((2, replicas - 1)), dma((2, replicas - 1)),
        dma((2, replicas - 1)), dma((2, members - 1)),
        dma((2, ticks, replicas, members - 1)), dma((2, ticks, replicas, members - 1)),
        dma((2, ticks - 1, replicas, members - 1)), dma((2, ticks - 1, replicas, 2)),
        dma((2, replicas - 1)),
    ]
    inputs_t, pool, act_t, sum_hidden, sum_grad, sum_up, out_t = pl.pallas_call(
        functools.partial(ticks_kernel, sections, tensors, replicas, own_p, ticks),
        out_shape=(
            shape((replicas, 2, own_p, saved), bf16),
            shape((replicas, saved, width_p), bf16),
            shape((replicas, hidden, saved), bf16),
            shape((replicas, saved, hidden), bf16),
            shape((replicas, saved, width_p), bf16),
            shape((replicas, saved, width_p), bf16),
            shape((replicas, 2, own_p, rows), bf16),
        ),
        in_specs=[hbm] * 8,
        out_specs=(vmem,) * 7,
        scratch_shapes=scratch,
        compiler_params=pltpu.CompilerParams(
            collective_id=0, has_side_effects=True, vmem_limit_bytes=60 * 1024 * 1024
        ),
        name="ticks",
    )(features, pool_own, crop_ids[0], seed, loss, proj, up, down)

    def trimmed(x, axis):
        if own == own_p:
            return x
        count = x.shape[axis] // own_p
        x = x.reshape(x.shape[:axis] + (count, own_p) + x.shape[axis + 1:])
        x = lax.slice_in_dim(x, 0, own, axis=axis + 1)
        return x.reshape(x.shape[:axis] + (count * own,) + x.shape[axis + 2:])

    kept = (act_t, sum_up, inputs_t, sum_grad, pool, sum_hidden)
    grad_down, grad_up, grad_proj = pl.pallas_call(
        functools.partial(tail_kernel, replicas),
        out_shape=(
            shape((hidden, width_p), bf16), shape((width_p, hidden), bf16),
            shape((2, own_p, width_p), bf16),
        ),
        in_specs=[pl.BlockSpec(memory_space=pltpu.SMEM)] + [hbm] * 6,
        out_specs=(hbm,) * 3,
        scratch_shapes=[pltpu.VMEM(x.shape, bf16) for x in kept] + [
            pltpu.VMEM((hidden, width_p), bf16), pltpu.VMEM((width_p, hidden), bf16),
            pltpu.VMEM((2, own_p, width_p), bf16),
            dma((6,)),
            dma((-(-hidden // 128) - (-width_p // 128) + 4,)),
        ],
        compiler_params=pltpu.CompilerParams(vmem_limit_bytes=60 * 1024 * 1024),
        name="tail",
    )(keep, *kept)
    grad_down = trimmed(grad_down, 1)[None]
    grad_up = trimmed(grad_up, 0)[None]
    grad_proj = trimmed(trimmed(grad_proj, 1), 2)[None]
    outgoing = trimmed(out_t, 2).transpose(3, 1, 0, 2).reshape(rows, 2, replicas * own)
    return grad_proj, grad_up, grad_down, outgoing[None]


def solution(mesh):
    in_specs = (
        P("section", "replica", None, "tensor"),
        P("section", "replica", None),
        P("section", "replica", None),
        P("section", "replica", "tensor"),
        P(None, "replica", "tensor"),
        P("section", None, ("tensor", "replica"), None),
        P("section", None, ("tensor", "replica")),
        P("section", ("tensor", "replica"), None),
    )
    out_specs = (
        P("section", None, ("tensor", "replica"), None),
        P("section", None, ("tensor", "replica")),
        P("section", ("tensor", "replica"), None),
        P("section", "replica", None, "tensor"),
    )
    return jax.shard_map(body, mesh=mesh, in_specs=in_specs, out_specs=out_specs, check_vma=False)
```

profile of v0, /device:TPU:12, one launch (start us, length us, event | category | flops | bytes accessed | tf_op | source)
XLA Modules:
  0.0 151.8 jit_solution(7541092610091520565)
XLA Ops:
  0.6 1.7 %copy.18 = bf16[2,2,352,128]{3,2,0,1:T(8,128)(2,1)} copy(bf16[2,2,352,128]{3,2,1,0:T(8,128)(2,1)} %bitcast.35) | data formatting | bytes 720896 | tf_op jit(solution)/shard_map/reshape | solution.py:394
  2.4 1.9 %copy.17 = bf16[3,2,352,128]{3,2,0,1:T(8,128)(2,1)} copy(bf16[3,2,352,128]{3,2,1,0:T(8,128)(2,1)} %bitcast.33) | data formatting | bytes 1081344 | tf_op jit(solution)/shard_map/reshape | solution.py:397
  4.3 139.5 %ticks.1 = (bf16[2,2,352,128]{3,2,1,0:T(8,128)(2,1)}, bf16[2,128,1408]{2,1,0:T(8,128)(2,1)}, bf16[2,768,128]{2,1,0:T(8,128)(2,1)}, bf16[2,128,768]{2,1,0:T(8,128...) custom-call(bf16[2,2,352,128]{3,2,1,0:T(8,128)(2,1)} %bitcast.32, ...), custom_call_target="tpu_custom_call" | custom-call | tf_op jit(solution)/shard_map/ticks/pallas_call | solution.py:428
  143.8 1.7 %copy.14 = bf16[128,2,2,352]{0,3,2,1:T(8,128)(2,1)} copy(bf16[128,2,2,352]{0,3,1,2:T(8,128)(2,1)} %bitcast.37) | data formatting | bytes 720896 | tf_op jit(solution)/shard_map/transpose | solution.py:477
  145.5 6.1 %tail.1 = (bf16[768,1408]{1,0:T(8,128)(2,1)}, bf16[1408,768]{1,0:T(8,128)(2,1)}, bf16[2,352,1408]{2,1,0:T(8,128)(2,1)}) custom-call(f32[1]{0:T(128)} %bitcast.keep_ref, bf16[2,768,128]{2,1,0:T(8,128)(2,1)} %get-tuple-element.14.act_hbm, bf16[2,128,1408]{2,1,0:T(8,128)(2,1)} %get-tuple-element.15.sum_up_hbm, ...), custom_call_target="tpu_custom_call" | custom-call | tf_op jit(solution)/shard_map/tail/pallas_call | solution.py:457
where the time goes:
time: 154 us; the launch traced here: 152 us
  Pallas kernels  146 us (95%)
  local copies, waits for them, and re-layouts  5.37 us (3%)
    pallas_call x1, Pallas kernels, body(): pl.pallas_call(functools.partial(ticks_kernel, sections, tensors, replica...  140 us
    pallas_call x1, Pallas kernels, body(): pl.pallas_call(functools.partial(tail_kernel, replicas), out_shape=(shape...  6.08 us

commit v1 on v0

v1 whole, which is shorter than its diff:
```python
import functools

import jax
import jax.numpy as jnp
from jax import lax
from jax.experimental import pallas as pl
from jax.experimental.pallas import tpu as pltpu
from jax.sharding import PartitionSpec as P

gelu_scale = 0.7978845608
gelu_cubic = 0.044715
bf16, f32 = jnp.bfloat16, jnp.float32
MESH = pl.DeviceIdType.MESH


def gelu_pair(pre_gelu):
    inner = gelu_scale * (pre_gelu + gelu_cubic * pre_gelu * pre_gelu * pre_gelu)
    tanh_part = jnp.tanh(inner)
    gelu_value = 0.5 * pre_gelu * (1.0 + tanh_part)
    gelu_slope = 0.5 * (1.0 + tanh_part) + 0.5 * pre_gelu * (
        1.0 - tanh_part * tanh_part
    ) * gelu_scale * (1.0 + 3.0 * gelu_cubic * pre_gelu * pre_gelu)
    return (gelu_value, gelu_slope)


def dot(a, b):
    return jnp.dot(a, b, preferred_element_type=f32)


def dot_nt(a, b):
    return lax.dot_general(a, b, (((1,), (1,)), ((), ())), preferred_element_type=f32)


def ticks_kernel(
    sections, tensors, replicas, own, ticks,
    inputs_hbm, pool_hbm, ids_hbm, seed_hbm, loss_hbm, proj_hbm, up_hbm, down_hbm,
    in_got, pool_out, act_out, hidden_out, grad_out, up_out, out,
    proj, up, down, loss_src, ids, loss_t, pool, pool_t, act_t,
    upstream, grads, hidden, part, relay, got, keep_part, own_part, slope_hi, slope_lo, slope,
    edge, edge_got, acc_hidden, acc_grad, acc_up, sum_hidden, sum_grad, sum_up,
    load_sem, out_sem, pool_sems, inputs_sems, ids_sems, loss_sems, seed_sems,
    part_sems, grad_sems, up_sems, edge_sems, outgoing_sems,
):
    members = tensors * replicas
    square = tensors == 2 and replicas == 2 and own % 32 == 0
    half = own // 2
    section = lax.axis_index("section")
    tensor = lax.axis_index("tensor")
    replica = lax.axis_index("replica")
    me = tensor * replicas + replica
    hidden_rows = down.shape[0]
    saved = pool.shape[1]
    last = ticks - 1
    along = (1 - tensor) * replicas + replica
    across = tensor * replicas + (1 - replica)
    far = (1 - tensor) * replicas + (1 - replica)

    def device(s, member):
        return {
            "section": s,
            "tensor": lax.div(member, replicas),
            "replica": lax.rem(member, replicas),
        }

    def member_at(by):
        return lax.rem(me + by, members)

    def replica_at(by):
        return lax.rem(replica + by, replicas)

    def slab_of(member):
        return pl.ds(pl.multiple_of(member * own, 16), own)

    def load(i, src, dst):
        copy = pltpu.make_async_copy(src, dst, load_sem.at[i])
        copy.start()
        return copy

    wide = pl.ds(pl.multiple_of(tensor * (replicas * own), 16), replicas * own)
    pairs = [
        (pool_hbm, pool.at[replica]), (seed_hbm, upstream.at[0, replica, wide]),
        (ids_hbm, ids.at[replica]), (up_hbm, up), (loss_hbm, loss_src),
        (loss_hbm.at[:, replica], loss_t.at[replica]), (down_hbm, down), (proj_hbm, proj),
    ]
    loads = [load(i, src, dst) for i, (src, dst) in enumerate(pairs)]
    ld_pool, ld_seed, ld_ids, ld_up, ld_loss, ld_loss_own, ld_down, ld_proj = loads

    barrier = pltpu.get_barrier_semaphore()
    above = lax.rem(section + 1, sections)
    below = lax.rem(section + sections - 1, sections)
    mirror = sections - 1 - section
    for by in range(1, members):
        pl.semaphore_signal(barrier, 1, device_id=device(section, member_at(by)), device_id_type=MESH)
    for other in (above, below, mirror):
        pl.semaphore_signal(barrier, 1, device_id=device(other, me), device_id_type=MESH)
    pl.semaphore_wait(barrier, members - 1 + 3)

    sent = []
    written = []

    def send(src, dst, sems, index, member):
        copy = pltpu.make_async_remote_copy(
            src_ref=src, dst_ref=dst, send_sem=sems.at[(0,) + index], recv_sem=sems.at[(1,) + index],
            device_id=device(section, member), device_id_type=MESH,
        )
        copy.start()
        sent.append(copy)
        return copy

    def over_replicas(src_of, dst, sems):
        return [
            send(src_of(replica_at(by)), dst, sems, (by - 1,), tensor * replicas + replica_at(by))
            for by in range(1, replicas)
        ]

    def write(src, dst):
        copy = pltpu.make_async_copy(src, dst, out_sem.at[len(written)])
        copy.start()
        written.append(copy)

    class Gather:
        def __init__(self, at, whole, sems, index):
            self.at, self.sems, self.index = at, sems, index
            if square:
                self.copies = [
                    self.put(me, h, i, to)
                    for i, (h, to) in enumerate(((0, along), (1, across), (1, along), (0, across)))
                ]
            else:
                self.copies = [
                    send(whole, whole, sems, index + (by - 1,), member_at(by))
                    for by in range(1, members)
                ]

        def put(self, member, h, i, to):
            ref = self.at(member, h)
            return send(ref, ref, self.sems, self.index + (i,), to)

        def forward(self):
            if square:
                self.copies[0].wait_recv()
                self.copies.append(self.put(along, 0, 4, across))
                self.copies[1].wait_recv()
                self.copies.append(self.put(across, 1, 5, along))

        def finish(self):
            for copy in self.copies[2 if square else 0:]:
                copy.wait_recv()

    def halves_of(ref):
        return lambda member, h: ref.at[pl.ds(pl.multiple_of(member * own + h * half, 16), half)]

    def seed_at(member, h):
        return upstream.at[0, lax.rem(member, replicas),
                           pl.ds(pl.multiple_of(lax.div(member, replicas) * (replicas * own) + h * own, 16), own)]

    slab = slab_of(me)
    ld_pool.wait()
    if square:
        mine = pl.ds(pl.multiple_of(tensor * (saved // 2), 16), saved // 2)
        own_pool = pool.at[replica, mine]
        pool_in = send(own_pool, own_pool, pool_sems, (0,), across)
    else:
        pool_in = over_replicas(lambda r: pool.at[replica], pool.at[replica], pool_sems)
    ld_ids.wait()
    ids_in = over_replicas(lambda r: ids.at[replica], ids.at[replica], ids_sems)
    ld_seed.wait()
    seed_in = Gather(seed_at, upstream.at[0, replica, wide], seed_sems, ())
    is_top = section == sections - 1

    step = 128

    def pre_slopes(r):
        def pre_at(start, size):
            cols = pl.ds(start, size)
            value, gelu_slope = gelu_pair(dot(pool[r], up[:, cols]).T)
            act_t[cols, pl.ds(pl.multiple_of(r * saved, 128), saved)] = value.astype(bf16)
            high = gelu_slope.astype(bf16)
            slope_hi[r, cols, :] = high
            slope_lo[r, cols, :] = (gelu_slope - high.astype(f32)).astype(bf16)

        @pl.loop(0, hidden_rows // step)
        def _(c):
            pre_at(pl.multiple_of(c * step, step), step)

        if hidden_rows % step:
            pre_at(hidden_rows - hidden_rows % step, hidden_rows % step)

    ld_up.wait()
    pre_slopes(replica)
    if square:
        pool_in.wait_recv()
        come = pool.at[1 - replica, mine]
        pool_over = send(come, come, pool_sems, (1,), along)
        seed_in.forward()
        pool_over.wait_recv()
        pre_slopes(1 - replica)
    else:
        for by in range(1, replicas):
            pool_in[by - 1].wait_recv()
            pre_slopes(lax.rem(replica + replicas - by, replicas))
    write(act_t, act_out)
    for copy in ids_in:
        copy.wait_recv()

    def picks(t, r):
        row = ids[r, pl.ds(t, 1), :]
        place_of = lax.broadcasted_iota(jnp.int32, (saved, row.shape[1]), 0)
        return jnp.where(place_of == row, 1.0, 0.0).astype(bf16)

    def pick_slope(t, r):
        chosen = picks(t, r)
        slope[r] = dot(slope_hi[r], chosen) + dot(slope_lo[r], chosen)

    for r in range(replicas):
        pick_slope(0, r)

    ld_down.wait()
    seed_in.finish()

    up_in, part_in, grad_in, edge_in = {}, {}, {}, {}

    def stage_hidden(t, r):
        if t > 0:
            up_in[t, r].finish()
        hidden[t, r] = (dot(down[...], upstream[t, r]) * slope[r]).astype(bf16)

        def partial(member):
            return dot(up[slab_of(member), :], hidden[t, r])

        if square:
            part[t, r, 0] = partial(far).astype(bf16)
            low, high = pl.ds(0, half), pl.ds(half, half)
            copies = [
                send(part.at[t, r, 0, low], relay.at[t, r, 0], part_sems, (t, r, 0), across),
                send(part.at[t, r, 0, high], relay.at[t, r, 1], part_sems, (t, r, 1), along),
            ]
            term = partial(along)
            part[t, r, 1, high] = term[half:].astype(bf16)
            copies.append(send(part.at[t, r, 1, high], got.at[t, r, 0, high], part_sems, (t, r, 2), along))
            keep_part[r, 0] = term[:half]
            term = partial(across)
            part[t, r, 2, low] = term[:half].astype(bf16)
            copies.append(send(part.at[t, r, 2, low], got.at[t, r, 1, low], part_sems, (t, r, 3), across))
            keep_part[r, 1] = term[half:]
        else:
            copies = []
            for by in range(1, members):
                to = member_at(by)
                part[t, r, by - 1] = partial(to).astype(bf16)
                copies.append(send(part.at[t, r, by - 1], got.at[t, r, by - 1], part_sems,
                                   (t, r, by - 1), to))
        own_part[r] = partial(me) + upstream[t, r, slab, :].astype(f32)
        part_in[t, r] = copies

    def stage_relay(t, r):
        if square:
            copies = part_in[t, r]
            for k, (to, start) in enumerate(((along, 0), (across, half))):
                rows = pl.ds(start, half)
                copies[k].wait_recv()
                part[t, r, k + 1, rows] = (keep_part[r, k] + relay[t, r, k].astype(f32)).astype(bf16)
                copies.append(send(part.at[t, r, k + 1, rows], got.at[t, r, k, rows], part_sems,
                                   (t, r, 4 + k), to))

    def stage_sum(t, r):
        for copy in part_in[t, r][2 if square else 0:]:
            copy.wait_recv()
        total = own_part[r]
        for k in range(got.shape[2]):
            total = total + got[t, r, k].astype(f32)
        grads[t, r, slab, :] = total.astype(bf16)
        grad_in[t, r] = Gather(halves_of(grads.at[t, r]), grads.at[t, r, slab], grad_sems, (t, r))

    def stage_project(t, r):
        grad_in[t, r].finish()
        edge[t, r, 0] = dot(proj[0], grads[t, r]).astype(bf16)
        if t == last:
            return
        down_copy = pltpu.make_async_remote_copy(
            src_ref=edge.at[t, r, 0], dst_ref=edge_got.at[t, r, 0],
            send_sem=edge_sems.at[0, t, r, 0], recv_sem=edge_sems.at[1, t, r, 0],
            device_id=device(below, me), device_id_type=MESH,
        )
        pl.when(section > 0)(down_copy.start)
        skip = pltpu.make_async_remote_copy(
            src_ref=edge.at[t, r, 1], dst_ref=edge_got.at[t, r, 1],
            send_sem=edge_sems.at[0, t, r, 1], recv_sem=edge_sems.at[1, t, r, 1],
            device_id=device(mirror, me), device_id_type=MESH,
        )

        @pl.when(section >= sections // 2)
        def _():
            edge[t, r, 1] = dot(proj[1], grads[t, r]).astype(bf16)
            skip.start()

        edge_in[t, r] = (down_copy, skip)

    def stage_next(t, r):
        down_copy, skip = edge_in[t, r]

        @pl.when(section < sections // 2)
        def _():
            down_copy.wait_recv()
            skip.wait_recv()
            summed = edge_got[t, r, 0].astype(f32) + edge_got[t, r, 1].astype(f32)
            upstream[t + 1, r, slab, :] = summed.astype(bf16)

        @pl.when((section >= sections // 2) & (section < sections - 1))
        def _():
            down_copy.wait_recv()
            upstream[t + 1, r, slab, :] = edge_got[t, r, 0]

        @pl.when(section == sections - 1)
        def _():
            upstream[t + 1, r, slab, :] = loss_t[r, t]

        up_in[t + 1, r] = Gather(halves_of(upstream.at[t + 1, r]), upstream.at[t + 1, r, slab], up_sems, (t, r))

    def add(t, r, acc, total, term):
        rows = pl.ds(r * saved, saved)
        value = term if t == 0 else acc[r] + term
        if t == last:
            total[rows, :] = value.astype(bf16)
        else:
            acc[r] = value

    every = range(replicas)
    to_last = []
    for t in range(ticks):
        for r in every:
            stage_hidden(t, r)
        if t == 0:
            ld_loss.wait()
            ld_loss_own.wait()
            loss_in = []
            for by in range(1, replicas):
                to = replica_at(by)
                loss_in.append(pltpu.make_async_remote_copy(
                    src_ref=loss_src.at[:, to], dst_ref=loss_t.at[replica],
                    send_sem=loss_sems.at[0, by - 1], recv_sem=loss_sems.at[1, by - 1],
                    device_id=device(section, tensor * replicas + to), device_id_type=MESH,
                ))
            for copy in loss_in:
                pl.when(is_top)(copy.start)
        for r in every:
            stage_relay(t, r)
            chosen = picks(t, r)
            add(t, r, acc_hidden, sum_hidden, dot_nt(chosen, hidden[t, r]))
            add(t, r, acc_up, sum_up, dot_nt(chosen, upstream[t, r]))
        if t == last:
            write(sum_hidden, hidden_out)
            write(sum_up, up_out)
        for r in every:
            stage_sum(t, r)
        if t < last:
            for r in every:
                pick_slope(t + 1, r)
        if t == 0:
            ld_proj.wait()
            for r in every:
                pool_t[:, pl.ds(r * saved, saved)] = pool[r].T
            write(pool_t, pool_out)
            for copy in loss_in:
                pl.when(is_top)(copy.wait_recv)
        for r in every:
            grad_in[t, r].forward()
        if t < last:
            for r in every:
                stage_project(t, r)
            if t == min(1, ticks - 1):
                inputs_in = over_replicas(lambda r: inputs_hbm.at[:, r], in_got.at[replica], inputs_sems)
            for r in every:
                stage_next(t, r)
            for r in every:
                add(t, r, acc_grad, sum_grad, dot_nt(picks(t, r), grads[t, r]))
            for r in every:
                up_in[t + 1, r].forward()

    outs = []
    for by in range(1, replicas):
        to = replica_at(by)
        for k in range(2):
            outs.append(pltpu.make_async_remote_copy(
                src_ref=edge.at[last, to, k], dst_ref=out.at[k, replica],
                send_sem=outgoing_sems.at[0, by - 1, k], recv_sem=outgoing_sems.at[1, by - 1, k],
                device_id=device(section, tensor * replicas + to), device_id_type=MESH,
            ))
    for r in every:
        grad_in[last, r].finish()
        for k in range(2):
            edge[last, r, k] = dot(proj[k], grads[last, r]).astype(bf16)
            for by in range(1, replicas):
                pl.when(replica_at(by) == r)(outs[2 * (by - 1) + k].start)
        add(last, r, acc_grad, sum_grad, dot_nt(picks(last, r), grads[last, r]))
    write(sum_grad, grad_out)
    write(edge.at[last, replica], out.at[:, replica])
    for copy in outs:
        copy.wait()
    for copy in inputs_in:
        copy.wait_recv()
    for copy in written:
        copy.wait()
    for copy in loss_in:
        pl.when(is_top)(copy.wait_send)
    for copy in sent:
        copy.wait_send()
    for key in edge_in:
        down_copy, skip = edge_in[key]
        pl.when(section > 0)(down_copy.wait_send)
        pl.when(section >= sections // 2)(skip.wait_send)


def tail_kernel(
    replicas, keep_ref, act_hbm, sum_up_hbm, pool_hbm, sum_hidden_hbm, inputs_hbm, in_got_hbm,
    sum_grad_hbm, outgoing_hbm,
    down_out, up_out, proj_out, outgoing_out,
    act, sum_up, pool, sum_hidden, inputs, sum_grad, outgoing, down_v, up_v, proj_v, load_sems, sems,
):
    replica = lax.axis_index("replica")
    saved = sum_up.shape[0] // replicas
    copies = []

    def lanes(r):
        return inputs.at[:, :, pl.ds(pl.multiple_of(r * saved, 128), saved)]

    pairs = [
        (act_hbm, act), (sum_up_hbm, sum_up), (pool_hbm, pool), (sum_hidden_hbm, sum_hidden),
        (sum_grad_hbm, sum_grad), (outgoing_hbm, outgoing),
        (inputs_hbm.at[:, replica], lanes(replica)),
    ]
    for by in range(1, replicas):
        r = lax.rem(replica + by, replicas)
        pairs.append((in_got_hbm.at[r], lanes(r)))
    loads = [
        pltpu.make_async_copy(src, dst, load_sems.at[i]) for i, (src, dst) in enumerate(pairs)
    ]
    for copy in loads:
        copy.start()

    def put(src, dst):
        copy = pltpu.make_async_copy(src, dst, sems.at[len(copies)])
        copy.start()
        copies.append(copy)

    def finish(a, b, rows, kept, out, scale=None):
        total = dot(a[rows], b[...])
        if scale is not None:
            total = total * scale
        kept.at[rows][...] = total.astype(bf16)
        put(kept.at[rows], out.at[rows])

    loads[0].wait()
    loads[1].wait()
    for start in range(0, down_v.shape[0], 128):
        finish(act, sum_up, pl.ds(start, min(128, down_v.shape[0] - start)), down_v, down_out)
    loads[2].wait()
    loads[3].wait()
    for start in range(0, up_v.shape[0], 128):
        finish(pool, sum_hidden, pl.ds(start, min(128, up_v.shape[0] - start)), up_v, up_out)
    loads[5].wait()
    put(outgoing, outgoing_out)
    loads[4].wait()
    for copy in loads[6:]:
        copy.wait()
    half = proj_v.shape[1] // 2
    for k in range(2):
        for start in (0, half):
            finish(inputs, sum_grad, (k, pl.ds(start, half)), proj_v, proj_out, keep_ref[0] if k else None)
    for copy in copies:
        copy.wait()


def body(pool_inputs, pool_mixed, crop_ids, incoming, loss_grads, w_proj, w_up, w_down):
    sections = lax.axis_size("section")
    tensors, replicas = lax.axis_size("tensor"), lax.axis_size("replica")
    members = tensors * replicas
    encoder = lax.axis_index("section") < sections // 2
    own = w_proj.shape[2]
    own_p = -(-own // 16) * 16
    rows, width = incoming.shape[1], w_up.shape[1]
    width_p = members * own_p
    hidden = w_up.shape[2]
    ticks = crop_ids.shape[1]
    saved = pool_mixed.shape[1]

    def padded(x, axis):
        if own == own_p:
            return x
        count = x.shape[axis] // own
        shape = x.shape[:axis] + (count, own) + x.shape[axis + 1:]
        fill = [(0, 0)] * (x.ndim + 1)
        fill[axis + 1] = (0, own_p - own)
        shape_p = x.shape[:axis] + (count * own_p,) + x.shape[axis + 1:]
        return jnp.pad(x.reshape(shape), fill).reshape(shape_p)

    proj = padded(padded(w_proj[0], 1), 2)
    up, down = padded(w_up[0], 0), padded(w_down[0], 1)
    pool_own = padded(pool_mixed[0], 1)
    keep = jnp.where(encoder, 0.0, 1.0).astype(f32)[None]
    features = pool_inputs[0].transpose(1, 2, 0).reshape(2, replicas, own, saved)
    features = padded(features, 2)
    seed = padded(incoming[0].T, 0)
    loss = loss_grads.transpose(0, 2, 1).reshape(ticks - 1, replicas, own, rows)
    loss = padded(loss, 2)

    shape = jax.ShapeDtypeStruct
    vmem = pl.BlockSpec(memory_space=pltpu.VMEM)
    hbm = pl.BlockSpec(memory_space=pl.ANY)
    dma = pltpu.SemaphoreType.DMA
    square = tensors == 2 and replicas == 2 and own_p % 32 == 0
    flows = 6 if square else members - 1
    terms = 2 if square else members - 1
    scratch = [
        pltpu.VMEM(proj.shape, bf16), pltpu.VMEM(up.shape, bf16), pltpu.VMEM(down.shape, bf16),
        pltpu.VMEM(loss.shape, bf16), pltpu.VMEM((replicas,) + crop_ids.shape[1:], jnp.int32),
        pltpu.VMEM((replicas, ticks - 1, own_p, rows), bf16),
        pltpu.VMEM((replicas, saved, width_p), bf16), pltpu.VMEM((width_p, replicas * saved), bf16),
        pltpu.VMEM((hidden, replicas * saved), bf16),
        pltpu.VMEM((ticks, replicas, width_p, rows), bf16),
        pltpu.VMEM((ticks, replicas, width_p, rows), bf16),
        pltpu.VMEM((ticks, replicas, hidden, rows), bf16),
        pltpu.VMEM((ticks, replicas, members - 1, own_p, rows), bf16),
        pltpu.VMEM((ticks, replicas, 2, own_p // 2, rows), bf16),
        pltpu.VMEM((ticks, replicas, terms, own_p, rows), bf16),
        pltpu.VMEM((replicas, 2, own_p // 2, rows), f32),
        pltpu.VMEM((replicas, own_p, rows), f32),
        pltpu.VMEM((replicas, hidden, saved), bf16), pltpu.VMEM((replicas, hidden, saved), bf16),
        pltpu.VMEM((replicas, hidden, rows), f32),
        pltpu.VMEM((ticks, replicas, 2, own_p, rows), bf16),
        pltpu.VMEM((ticks - 1, replicas, 2, own_p, rows), bf16),
        pltpu.VMEM((replicas, saved, hidden), f32), pltpu.VMEM((replicas, saved, width_p), f32),
        pltpu.VMEM((replicas, saved, width_p), f32),
        pltpu.VMEM((replicas * saved, hidden), bf16), pltpu.VMEM((replicas * saved, width_p), bf16),
        pltpu.VMEM((replicas * saved, width_p), bf16),
        dma((8,)), dma((6,)), dma((2, max(2, replicas - 1))), dma((2, replicas - 1)),
        dma((2, replicas - 1)), dma((2, replicas - 1)), dma((2, flows)),
        dma((2, ticks, replicas, flows)), dma((2, ticks, replicas, flows)),
        dma((2, ticks - 1, replicas, flows)), dma((2, ticks - 1, replicas, 2)),
        dma((2, replicas - 1, 2)),
    ]
    in_got, pool_t, act_t, sum_hidden, sum_grad, sum_up, out = pl.pallas_call(
        functools.partial(ticks_kernel, sections, tensors, replicas, own_p, ticks),
        out_shape=(
            shape((replicas, 2, own_p, saved), bf16),
            shape((width_p, replicas * saved), bf16),
            shape((hidden, replicas * saved), bf16),
            shape((replicas * saved, hidden), bf16),
            shape((replicas * saved, width_p), bf16),
            shape((replicas * saved, width_p), bf16),
            shape((2, replicas, own_p, rows), bf16),
        ),
        in_specs=[hbm] * 8,
        out_specs=(hbm,) * 7,
        scratch_shapes=scratch,
        compiler_params=pltpu.CompilerParams(
            collective_id=0, has_side_effects=True, vmem_limit_bytes=60 * 1024 * 1024
        ),
        name="ticks",
    )(features, pool_own, crop_ids[0], seed, loss, proj, up, down)

    def trimmed(x, axis):
        if own == own_p:
            return x
        count = x.shape[axis] // own_p
        x = x.reshape(x.shape[:axis] + (count, own_p) + x.shape[axis + 1:])
        x = lax.slice_in_dim(x, 0, own, axis=axis + 1)
        return x.reshape(x.shape[:axis] + (count * own,) + x.shape[axis + 2:])

    kept = (act_t, sum_up, pool_t, sum_hidden)
    grad_down, grad_up, grad_proj, outgoing = pl.pallas_call(
        functools.partial(tail_kernel, replicas),
        out_shape=(
            shape((hidden, width_p), bf16), shape((width_p, hidden), bf16),
            shape((2, own_p, width_p), bf16), shape(out.shape, bf16),
        ),
        in_specs=[pl.BlockSpec(memory_space=pltpu.SMEM)] + [hbm] * 8,
        out_specs=(hbm,) * 4,
        scratch_shapes=[pltpu.VMEM(x.shape, bf16) for x in kept] + [
            pltpu.VMEM((2, own_p, replicas * saved), bf16), pltpu.VMEM(sum_grad.shape, bf16),
            pltpu.VMEM(out.shape, bf16),
            pltpu.VMEM((hidden, width_p), bf16), pltpu.VMEM((width_p, hidden), bf16),
            pltpu.VMEM((2, own_p, width_p), bf16),
            dma((6 + replicas,)),
            dma((-(-hidden // 128) - (-width_p // 128) + 5,)),
        ],
        compiler_params=pltpu.CompilerParams(vmem_limit_bytes=60 * 1024 * 1024),
        name="tail",
    )(keep, *kept, features, in_got, sum_grad, out)
    grad_down = trimmed(grad_down, 1)[None]
    grad_up = trimmed(grad_up, 0)[None]
    grad_proj = trimmed(trimmed(grad_proj, 1), 2)[None]
    outgoing = trimmed(outgoing, 2).reshape(2, replicas * own, rows).transpose(2, 0, 1)
    return grad_proj, grad_up, grad_down, outgoing[None]


def solution(mesh):
    in_specs = (
        P("section", "replica", None, "tensor"),
        P("section", "replica", None),
        P("section", "replica", None),
        P("section", "replica", "tensor"),
        P(None, "replica", "tensor"),
        P("section", None, ("tensor", "replica"), None),
        P("section", None, ("tensor", "replica")),
        P("section", ("tensor", "replica"), None),
    )
    out_specs = (
        P("section", None, ("tensor", "replica"), None),
        P("section", None, ("tensor", "replica")),
        P("section", ("tensor", "replica"), None),
        P("section", "replica", None, "tensor"),
    )
    return jax.shard_map(body, mesh=mesh, in_specs=in_specs, out_specs=out_specs, check_vma=False)
```

time: 154 us -> 133 us (0.86)
  the two profiles are of different devices: /device:TPU:12 before, /device:TPU:0 now
where the time goes in v1:
time: 133 us
  Pallas kernels  132 us (99%)
    pallas_call x1, Pallas kernels, body(): pl.pallas_call(functools.partial(ticks_kernel, sections, tensors, replica...  128 us
    pallas_call x1, Pallas kernels, body(): pl.pallas_call(functools.partial(tail_kernel, replicas), out_shape=(shape...  4.58 us

profile of v1, /device:TPU:0, one launch (start us, length us, event | category | flops | bytes accessed | tf_op | source)
XLA Modules:
  0.0 132.9 jit_solution(11998558938725907914)
XLA Ops:
  0.6 127.5 %ticks.1 = (bf16[2,2,352,128]{3,2,1,0:T(8,128)(2,1)}, bf16[1408,256]{1,0:T(8,128)(2,1)}, bf16[768,256]{1,0:T(8,128)(2,1)}, bf16[256,768]{1,0:T(8,128)(2,1)}, bf1...) custom-call(bf16[2,2,352,128]{3,2,1,0:T(8,128)(2,1)} %bitcast.28, ...), custom_call_target="tpu_custom_call" | custom-call | tf_op jit(solution)/shard_map/ticks/pallas_call | solution.py:542
  128.2 4.6 %tail.1 = (bf16[768,1408]{1,0:T(8,128)(2,1)}, bf16[1408,768]{1,0:T(8,128)(2,1)}, bf16[2,352,1408]{2,1,0:T(8,128)(2,1)}, bf16[2,2,352,128]{3,2,1,0:T(8,128)(2,1)}) custom-call(f32[1]{0:T(128)} %bitcast.keep_ref, bf16[768,256]{1,0:T(8,128)(2,1)} %get-tuple-element.15.act_hbm, bf16[256,1408]{1,0:T(8,128)(2,1)} %get-tuple-element.16.sum_up_hbm, ...), custom_call_target="tpu_custom_call" | custom-call | tf_op jit(solution)/shard_map/tail/pallas_call | solution.py:571

commit v2 on v1

--- a/solution.py
+++ b/solution.py
@@ -38,8 +38,8 @@
     proj, up, down, loss_src, ids, loss_t, pool, pool_t, act_t,
     upstream, grads, hidden, part, relay, got, keep_part, own_part, slope_hi, slope_lo, slope,
     edge, edge_got, acc_hidden, acc_grad, acc_up, sum_hidden, sum_grad, sum_up,
-    load_sem, out_sem, pool_sems, inputs_sems, ids_sems, loss_sems, seed_sems,
-    part_sems, grad_sems, up_sems, edge_sems, outgoing_sems,
+    load_sem, out_sem, send_sems, pool_sems, inputs_sems, ids_sems, loss_sems, seed_sems,
+    part_sems, grad_sems, up_sems, edge_sems, outgoing_sems, up_near,
 ):
     members = tensors * replicas
     square = tensors == 2 and replicas == 2 and own % 32 == 0
@@ -71,19 +71,27 @@
     def slab_of(member):
         return pl.ds(pl.multiple_of(member * own, 16), own)
 
-    def load(i, src, dst):
-        copy = pltpu.make_async_copy(src, dst, load_sem.at[i])
+    loads = []
+
+    def load(src, dst):
+        copy = pltpu.make_async_copy(src, dst, load_sem.at[len(loads)])
         copy.start()
+        loads.append(copy)
         return copy
 
     wide = pl.ds(pl.multiple_of(tensor * (replicas * own), 16), replicas * own)
-    pairs = [
-        (pool_hbm, pool.at[replica]), (seed_hbm, upstream.at[0, replica, wide]),
-        (ids_hbm, ids.at[replica]), (up_hbm, up), (loss_hbm, loss_src),
-        (loss_hbm.at[:, replica], loss_t.at[replica]), (down_hbm, down), (proj_hbm, proj),
-    ]
-    loads = [load(i, src, dst) for i, (src, dst) in enumerate(pairs)]
-    ld_pool, ld_seed, ld_ids, ld_up, ld_loss, ld_loss_own, ld_down, ld_proj = loads
+    ld_pool = load(pool_hbm, pool.at[replica])
+    ld_seed = load(seed_hbm, upstream.at[0, replica, wide])
+    ld_ids = load(ids_hbm, ids.at[replica])
+    ld_up = load(up_hbm, up)
+    ld_down = load(down_hbm, down)
+    near = []
+    if square:
+        for i, member in enumerate((far, along, across, me)):
+            near.append(load(up_hbm.at[slab_of(member)], up_near.at[pl.ds(i * own, own)]))
+    ld_loss = load(loss_hbm, loss_src)
+    ld_loss_own = load(loss_hbm.at[:, replica], loss_t.at[replica])
+    ld_proj = load(proj_hbm, proj)
 
     barrier = pltpu.get_barrier_semaphore()
     above = lax.rem(section + 1, sections)
@@ -95,23 +103,28 @@
         pl.semaphore_signal(barrier, 1, device_id=device(other, me), device_id_type=MESH)
     pl.semaphore_wait(barrier, members - 1 + 3)
 
-    sent = []
     written = []
-
-    def send(src, dst, sems, index, member):
-        copy = pltpu.make_async_remote_copy(
-            src_ref=src, dst_ref=dst, send_sem=sems.at[(0,) + index], recv_sem=sems.at[(1,) + index],
-            device_id=device(section, member), device_id_type=MESH,
+    POOL, IDS, SEED, PART, GRAD, UP, INPUTS, DOWN, SKIP, LOSS, OUT = range(11)
+
+    def remote(src, dst, kind, recv_sem, s, member):
+        return pltpu.make_async_remote_copy(
+            src_ref=src, dst_ref=dst, send_sem=send_sems.at[kind], recv_sem=recv_sem,
+            device_id=device(s, member), device_id_type=MESH,
         )
+
+    def send(src, dst, kind, recv_sem, member):
+        copy = remote(src, dst, kind, recv_sem, section, member)
         copy.start()
-        sent.append(copy)
         return copy
 
-    def over_replicas(src_of, dst, sems):
+    def over_replicas(src_of, dst, kind, sems):
         return [
-            send(src_of(replica_at(by)), dst, sems, (by - 1,), tensor * replicas + replica_at(by))
+            send(src_of(replica_at(by)), dst, kind, sems.at[by - 1], tensor * replicas + replica_at(by))
             for by in range(1, replicas)
         ]
+
+    def all_sent(kind, ref):
+        pltpu.make_async_copy(ref, ref, send_sems.at[kind]).wait()
 
     def write(src, dst):
         copy = pltpu.make_async_copy(src, dst, out_sem.at[len(written)])
@@ -119,22 +132,23 @@
         written.append(copy)
 
     class Gather:
-        def __init__(self, at, whole, sems, index):
-            self.at, self.sems, self.index = at, sems, index
+        def __init__(self, at, whole, kind, sems):
+            self.at, self.kind, self.sems = at, kind, sems
             if square:
-                self.copies = [
-                    self.put(me, h, i, to)
-                    for i, (h, to) in enumerate(((0, along), (1, across), (1, along), (0, across)))
-                ]
+                self.copies = [self.put(me, 0, 0, along), self.put(me, 1, 1, across)]
             else:
                 self.copies = [
-                    send(whole, whole, sems, index + (by - 1,), member_at(by))
+                    send(whole, whole, kind, sems.at[by - 1], member_at(by))
                     for by in range(1, members)
                 ]
 
         def put(self, member, h, i, to):
             ref = self.at(member, h)
-            return send(ref, ref, self.sems, self.index + (i,), to)
+            return send(ref, ref, self.kind, self.sems.at[i], to)
+
+        def follow(self):
+            if square:
+                self.copies += [self.put(me, 1, 2, along), self.put(me, 0, 3, across)]
 
         def forward(self):
             if square:
@@ -155,20 +169,29 @@
                            pl.ds(pl.multiple_of(lax.div(member, replicas) * (replicas * own) + h * own, 16), own)]
 
     slab = slab_of(me)
+    low, high = pl.ds(0, half), pl.ds(half, half)
     ld_pool.wait()
+    pieces = 2
     if square:
-        mine = pl.ds(pl.multiple_of(tensor * (saved // 2), 16), saved // 2)
-        own_pool = pool.at[replica, mine]
-        pool_in = send(own_pool, own_pool, pool_sems, (0,), across)
+        rows = saved // (2 * pieces)
+
+        def piece(r, p):
+            return pool.at[r, pl.ds(pl.multiple_of((tensor * pieces + p) * rows, 8), rows)]
+
+        pool_in = [
+            send(piece(replica, p), piece(replica, p), POOL, pool_sems.at[p], across)
+            for p in range(pieces)
+        ]
     else:
-        pool_in = over_replicas(lambda r: pool.at[replica], pool.at[replica], pool_sems)
+        pool_in = over_replicas(lambda r: pool.at[replica], pool.at[replica], POOL, pool_sems)
+    ld_seed.wait()
+    seed_in = Gather(seed_at, upstream.at[0, replica, wide], SEED, seed_sems)
+    seed_in.follow()
     ld_ids.wait()
-    ids_in = over_replicas(lambda r: ids.at[replica], ids.at[replica], ids_sems)
-    ld_seed.wait()
-    seed_in = Gather(seed_at, upstream.at[0, replica, wide], seed_sems, ())
+    ids_in = over_replicas(lambda r: ids.at[replica], ids.at[replica], IDS, ids_sems)
     is_top = section == sections - 1
 
-    step = 128
+    step = 256 if hidden_rows % 256 == 0 else 128
 
     def pre_slopes(r):
         def pre_at(start, size):
@@ -189,11 +212,14 @@
     ld_up.wait()
     pre_slopes(replica)
     if square:
-        pool_in.wait_recv()
-        come = pool.at[1 - replica, mine]
-        pool_over = send(come, come, pool_sems, (1,), along)
+        pool_over = []
+        for p in range(pieces):
+            pool_in[p].wait_recv()
+            come = piece(1 - replica, p)
+            pool_over.append(send(come, come, POOL, pool_sems.at[pieces + p], along))
         seed_in.forward()
-        pool_over.wait_recv()
+        for copy in pool_over:
+            copy.wait_recv()
         pre_slopes(1 - replica)
     else:
         for by in range(1, replicas):
@@ -216,6 +242,8 @@
         pick_slope(0, r)
 
     ld_down.wait()
+    for copy in near:
+        copy.wait()
     seed_in.finish()
 
     up_in, part_in, grad_in, edge_in = {}, {}, {}, {}
@@ -224,44 +252,42 @@
         if t > 0:
             up_in[t, r].finish()
         hidden[t, r] = (dot(down[...], upstream[t, r]) * slope[r]).astype(bf16)
-
-        def partial(member):
-            return dot(up[slab_of(member), :], hidden[t, r])
-
         if square:
-            part[t, r, 0] = partial(far).astype(bf16)
-            low, high = pl.ds(0, half), pl.ds(half, half)
-            copies = [
-                send(part.at[t, r, 0, low], relay.at[t, r, 0], part_sems, (t, r, 0), across),
-                send(part.at[t, r, 0, high], relay.at[t, r, 1], part_sems, (t, r, 1), along),
+            part[t, r, 0] = dot(up_near[:own, :], hidden[t, r]).astype(bf16)
+            part_in[t, r] = [
+                send(part.at[t, r, 0, low], relay.at[t, r, 0], PART, part_sems.at[r, 0], across),
+                send(part.at[t, r, 0, high], relay.at[t, r, 1], PART, part_sems.at[r, 1], along),
             ]
-            term = partial(along)
-            part[t, r, 1, high] = term[half:].astype(bf16)
-            copies.append(send(part.at[t, r, 1, high], got.at[t, r, 0, high], part_sems, (t, r, 2), along))
-            keep_part[r, 0] = term[:half]
-            term = partial(across)
-            part[t, r, 2, low] = term[:half].astype(bf16)
-            copies.append(send(part.at[t, r, 2, low], got.at[t, r, 1, low], part_sems, (t, r, 3), across))
-            keep_part[r, 1] = term[half:]
+
+    def stage_parts(t, r):
+        if square:
+            near_terms = dot(up_near[own:, :], hidden[t, r])
+            part[t, r, 1, high] = near_terms[half:own].astype(bf16)
+            part[t, r, 2, low] = near_terms[own:own + half].astype(bf16)
+            part_in[t, r] += [
+                send(part.at[t, r, 1, high], got.at[t, r, 0, high], PART, part_sems.at[r, 2], along),
+                send(part.at[t, r, 2, low], got.at[t, r, 1, low], PART, part_sems.at[r, 3], across),
+            ]
+            keep_part[r, 0] = near_terms[:half]
+            keep_part[r, 1] = near_terms[own + half:2 * own]
+            own_term = near_terms[2 * own:]
         else:
-            copies = []
+            part_in[t, r] = []
             for by in range(1, members):
                 to = member_at(by)
-                part[t, r, by - 1] = partial(to).astype(bf16)
-                copies.append(send(part.at[t, r, by - 1], got.at[t, r, by - 1], part_sems,
-                                   (t, r, by - 1), to))
-        own_part[r] = partial(me) + upstream[t, r, slab, :].astype(f32)
-        part_in[t, r] = copies
+                part[t, r, by - 1] = dot(up[slab_of(to), :], hidden[t, r]).astype(bf16)
+                part_in[t, r].append(send(part.at[t, r, by - 1], got.at[t, r, by - 1], PART,
+                                          part_sems.at[r, by - 1], to))
+            own_term = dot(up[slab, :], hidden[t, r])
+        own_part[r] = own_term + upstream[t, r, slab, :].astype(f32)
 
     def stage_relay(t, r):
         if square:
-            copies = part_in[t, r]
-            for k, (to, start) in enumerate(((along, 0), (across, half))):
-                rows = pl.ds(start, half)
-                copies[k].wait_recv()
+            for k, (to, rows) in enumerate(((along, low), (across, high))):
+                part_in[t, r][k].wait_recv()
                 part[t, r, k + 1, rows] = (keep_part[r, k] + relay[t, r, k].astype(f32)).astype(bf16)
-                copies.append(send(part.at[t, r, k + 1, rows], got.at[t, r, k, rows], part_sems,
-                                   (t, r, 4 + k), to))
+                part_in[t, r].append(send(part.at[t, r, k + 1, rows], got.at[t, r, k, rows], PART,
+                                          part_sems.at[r, 4 + k], to))
 
     def stage_sum(t, r):
         for copy in part_in[t, r][2 if square else 0:]:
@@ -270,24 +296,16 @@
         for k in range(got.shape[2]):
             total = total + got[t, r, k].astype(f32)
         grads[t, r, slab, :] = total.astype(bf16)
-        grad_in[t, r] = Gather(halves_of(grads.at[t, r]), grads.at[t, r, slab], grad_sems, (t, r))
+        grad_in[t, r] = Gather(halves_of(grads.at[t, r]), grads.at[t, r, slab], GRAD, grad_sems.at[r])
 
     def stage_project(t, r):
         grad_in[t, r].finish()
         edge[t, r, 0] = dot(proj[0], grads[t, r]).astype(bf16)
         if t == last:
             return
-        down_copy = pltpu.make_async_remote_copy(
-            src_ref=edge.at[t, r, 0], dst_ref=edge_got.at[t, r, 0],
-            send_sem=edge_sems.at[0, t, r, 0], recv_sem=edge_sems.at[1, t, r, 0],
-            device_id=device(below, me), device_id_type=MESH,
-        )
+        down_copy = remote(edge.at[t, r, 0], edge_got.at[t, r, 0], DOWN, edge_sems.at[t, r, 0], below, me)
         pl.when(section > 0)(down_copy.start)
-        skip = pltpu.make_async_remote_copy(
-            src_ref=edge.at[t, r, 1], dst_ref=edge_got.at[t, r, 1],
-            send_sem=edge_sems.at[0, t, r, 1], recv_sem=edge_sems.at[1, t, r, 1],
-            device_id=device(mirror, me), device_id_type=MESH,
-        )
+        skip = remote(edge.at[t, r, 1], edge_got.at[t, r, 1], SKIP, edge_sems.at[t, r, 1], mirror, me)
 
         @pl.when(section >= sections // 2)
         def _():
@@ -311,11 +329,14 @@
             down_copy.wait_recv()
             upstream[t + 1, r, slab, :] = edge_got[t, r, 0]
 
-        @pl.when(section == sections - 1)
+        @pl.when(is_top)
         def _():
+            if r == 0:
+                for copy in loss_in[t]:
+                    copy.wait_recv()
             upstream[t + 1, r, slab, :] = loss_t[r, t]
 
-        up_in[t + 1, r] = Gather(halves_of(upstream.at[t + 1, r]), upstream.at[t + 1, r, slab], up_sems, (t, r))
+        up_in[t + 1, r] = Gather(halves_of(upstream.at[t + 1, r]), upstream.at[t + 1, r, slab], UP, up_sems.at[r])
 
     def add(t, r, acc, total, term):
         rows = pl.ds(r * saved, saved)
@@ -325,90 +346,104 @@
         else:
             acc[r] = value
 
+    def settle(t, r):
+        chosen = picks(t, r)
+        add(t, r, acc_hidden, sum_hidden, dot_nt(chosen, hidden[t, r]))
+        add(t, r, acc_up, sum_up, dot_nt(chosen, upstream[t, r]))
+
     every = range(replicas)
-    to_last = []
+    loss_in, inputs_in = [], []
+    slices = [(k, rows) for k in range(2) for rows in (low, pl.ds(half, own - half))]
     for t in range(ticks):
         for r in every:
             stage_hidden(t, r)
-        if t == 0:
-            ld_loss.wait()
-            ld_loss_own.wait()
-            loss_in = []
-            for by in range(1, replicas):
-                to = replica_at(by)
-                loss_in.append(pltpu.make_async_remote_copy(
-                    src_ref=loss_src.at[:, to], dst_ref=loss_t.at[replica],
-                    send_sem=loss_sems.at[0, by - 1], recv_sem=loss_sems.at[1, by - 1],
-                    device_id=device(section, tensor * replicas + to), device_id_type=MESH,
-                ))
-            for copy in loss_in:
+            if r > 0:
+                stage_relay(t, r - 1)
+            stage_parts(t, r)
+        if t < last:
+            if t == 0:
+                ld_loss.wait()
+                ld_loss_own.wait()
+            loss_in.append([
+                remote(loss_src.at[t, replica_at(by)], loss_t.at[replica, t], LOSS,
+                       loss_sems.at[t, by - 1], section, tensor * replicas + replica_at(by))
+                for by in range(1, replicas)
+            ])
+            for copy in loss_in[t]:
                 pl.when(is_top)(copy.start)
+        settle(t, 0)
+        stage_relay(t, replicas - 1)
         for r in every:
-            stage_relay(t, r)
-            chosen = picks(t, r)
-            add(t, r, acc_hidden, sum_hidden, dot_nt(chosen, hidden[t, r]))
-            add(t, r, acc_up, sum_up, dot_nt(chosen, upstream[t, r]))
+            stage_sum(t, r)
+            if r == 0:
+                grad_in[t, r].follow()
+            if r + 1 < replicas:
+                settle(t, r + 1)
         if t == last:
             write(sum_hidden, hidden_out)
             write(sum_up, up_out)
-        for r in every:
-            stage_sum(t, r)
-        if t < last:
+        else:
             for r in every:
                 pick_slope(t + 1, r)
-        if t == 0:
-            ld_proj.wait()
-            for r in every:
-                pool_t[:, pl.ds(r * saved, saved)] = pool[r].T
-            write(pool_t, pool_out)
-            for copy in loss_in:
-                pl.when(is_top)(copy.wait_recv)
         for r in every:
             grad_in[t, r].forward()
-        if t < last:
-            for r in every:
-                stage_project(t, r)
-            if t == min(1, ticks - 1):
-                inputs_in = over_replicas(lambda r: inputs_hbm.at[:, r], in_got.at[replica], inputs_sems)
-            for r in every:
-                stage_next(t, r)
-            for r in every:
-                add(t, r, acc_grad, sum_grad, dot_nt(picks(t, r), grads[t, r]))
-            for r in every:
-                up_in[t + 1, r].forward()
-
-    outs = []
-    for by in range(1, replicas):
-        to = replica_at(by)
-        for k in range(2):
-            outs.append(pltpu.make_async_remote_copy(
-                src_ref=edge.at[last, to, k], dst_ref=out.at[k, replica],
-                send_sem=outgoing_sems.at[0, by - 1, k], recv_sem=outgoing_sems.at[1, by - 1, k],
-                device_id=device(section, tensor * replicas + to), device_id_type=MESH,
-            ))
+            if r + 1 < replicas:
+                grad_in[t, r + 1].follow()
+            if t == 0:
+                pool_t[:, pl.ds(r * saved, saved)] = pool[r].T
+        if t == 0:
+            write(pool_t, pool_out)
+            ld_proj.wait()
+        if t == last:
+            break
+        for i, (k, rows) in enumerate(slices):
+            if i * last // len(slices) == t:
+                inputs_in += over_replicas(lambda r: inputs_hbm.at[k, r, rows], in_got.at[replica, k, rows],
+                                           INPUTS, inputs_sems.at[i])
+        for r in every:
+            stage_project(t, r)
+        for r in every:
+            stage_next(t, r)
+            if r == 0:
+                up_in[t + 1, r].follow()
+        for r in every:
+            add(t, r, acc_grad, sum_grad, dot_nt(picks(t, r), grads[t, r]))
+            up_in[t + 1, r].forward()
+            if r + 1 < replicas:
+                up_in[t + 1, r + 1].follow()
+
+    outs = [
+        [
+            remote(edge.at[last, replica_at(by), k], out.at[k, replica], OUT,
+                   outgoing_sems.at[by - 1, k], section, tensor * replicas + replica_at(by))
+            for k in range(2)
+        ]
+        for by in range(1, replicas)
+    ]
     for r in every:
         grad_in[last, r].finish()
         for k in range(2):
             edge[last, r, k] = dot(proj[k], grads[last, r]).astype(bf16)
             for by in range(1, replicas):
-                pl.when(replica_at(by) == r)(outs[2 * (by - 1) + k].start)
+                pl.when(replica_at(by) == r)(outs[by - 1][k].start)
         add(last, r, acc_grad, sum_grad, dot_nt(picks(last, r), grads[last, r]))
     write(sum_grad, grad_out)
     write(edge.at[last, replica], out.at[:, replica])
-    for copy in outs:
-        copy.wait()
-    for copy in inputs_in:
+    for copy in inputs_in + [copy for pair in outs for copy in pair]:
         copy.wait_recv()
     for copy in written:
         copy.wait()
-    for copy in loss_in:
-        pl.when(is_top)(copy.wait_send)
-    for copy in sent:
-        copy.wait_send()
-    for key in edge_in:
-        down_copy, skip = edge_in[key]
-        pl.when(section > 0)(down_copy.wait_send)
-        pl.when(section >= sections // 2)(skip.wait_send)
+    all_sent(POOL, pool.at[pl.ds(0, replicas - 1)])
+    all_sent(IDS, ids.at[pl.ds(0, replicas - 1)])
+    all_sent(SEED, part.at[0])
+    all_sent(PART, part)
+    all_sent(GRAD, part)
+    all_sent(UP, part.at[pl.ds(0, last)])
+    all_sent(INPUTS, in_got.at[pl.ds(0, replicas - 1)])
+    all_sent(OUT, edge.at[last, pl.ds(0, replicas - 1)])
+    pl.when(section > 0)(lambda: all_sent(DOWN, edge_got.at[:, :, 0]))
+    pl.when(section >= sections // 2)(lambda: all_sent(SKIP, edge_got.at[:, :, 1]))
+    pl.when(is_top)(lambda: all_sent(LOSS, loss_t.at[pl.ds(0, replicas - 1)]))
 
 
 def tail_kernel(
@@ -533,11 +568,11 @@
         pltpu.VMEM((replicas, saved, width_p), f32),
         pltpu.VMEM((replicas * saved, hidden), bf16), pltpu.VMEM((replicas * saved, width_p), bf16),
         pltpu.VMEM((replicas * saved, width_p), bf16),
-        dma((8,)), dma((6,)), dma((2, max(2, replicas - 1))), dma((2, replicas - 1)),
-        dma((2, replicas - 1)), dma((2, replicas - 1)), dma((2, flows)),
-        dma((2, ticks, replicas, flows)), dma((2, ticks, replicas, flows)),
-        dma((2, ticks - 1, replicas, flows)), dma((2, ticks - 1, replicas, 2)),
-        dma((2, replicas - 1, 2)),
+        dma((12,)), dma((6,)), dma((11,)), dma((max(4, replicas - 1),)), dma((4, replicas - 1)),
+        dma((replicas - 1,)), dma((ticks - 1, replicas - 1)), dma((flows,)),
+        dma((replicas, flows)), dma((replicas, flows)), dma((replicas, flows)),
+        dma((ticks - 1, replicas, 2)), dma((replicas - 1, 2)),
+        pltpu.VMEM(up.shape if square else (16, 128), bf16),
     ]
     in_got, pool_t, act_t, sum_hidden, sum_grad, sum_up, out = pl.pallas_call(
         functools.partial(ticks_kernel, sections, tensors, replicas, own_p, ticks),

time: 133 us -> 119 us (0.89)
  the two profiles are of different devices: /device:TPU:0 before, /device:TPU:12 now
where the time goes in v2:
time: 119 us
  Pallas kernels  118 us (99%)
    pallas_call x1, Pallas kernels, body(): pl.pallas_call(functools.partial(ticks_kernel, sections, tensors, replica...  114 us
    pallas_call x1, Pallas kernels, body(): pl.pallas_call(functools.partial(tail_kernel, replicas), out_shape=(shape...  4.59 us

profile of v2, /device:TPU:12, one launch (start us, length us, event | category | flops | bytes accessed | tf_op | source)
XLA Modules:
  0.0 119.0 jit_solution(8750916649454542853)
XLA Ops:
  0.6 113.6 %ticks.1 = (bf16[2,2,352,128]{3,2,1,0:T(8,128)(2,1)}, bf16[1408,256]{1,0:T(8,128)(2,1)}, bf16[768,256]{1,0:T(8,128)(2,1)}, bf16[256,768]{1,0:T(8,128)(2,1)}, bf1...) custom-call(bf16[2,2,352,128]{3,2,1,0:T(8,128)(2,1)} %bitcast.28, ...), custom_call_target="tpu_custom_call" | custom-call | tf_op jit(solution)/shard_map/ticks/pallas_call | solution.py:577
  114.3 4.6 %tail.1 = (bf16[768,1408]{1,0:T(8,128)(2,1)}, bf16[1408,768]{1,0:T(8,128)(2,1)}, bf16[2,352,1408]{2,1,0:T(8,128)(2,1)}, bf16[2,2,352,128]{3,2,1,0:T(8,128)(2,1)}) custom-call(f32[1]{0:T(128)} %bitcast.keep_ref, bf16[768,256]{1,0:T(8,128)(2,1)} %get-tuple-element.15.act_hbm, bf16[256,1408]{1,0:T(8,128)(2,1)} %get-tuple-element.16.sum_up_hbm, ...), custom_call_target="tpu_custom_call" | custom-call | tf_op jit(solution)/shard_map/tail/pallas_call | solution.py:606

commit v3 on v2

--- a/solution.py
+++ b/solution.py
@@ -53,7 +53,6 @@
     last = ticks - 1
     along = (1 - tensor) * replicas + replica
     across = tensor * replicas + (1 - replica)
-    far = (1 - tensor) * replicas + (1 - replica)
 
     def device(s, member):
         return {
@@ -78,6 +77,15 @@
         copy.start()
         loads.append(copy)
         return copy
+
+    near_order = {1: ((0, 0), (1, 0), (0, 1), (1, 1)), 0: ((0, 0), (0, 1), (1, 0), (1, 1))}
+
+    def term(k, p, side):
+        if k == 0:
+            member = lax.rem(tensor + side, tensors) * replicas + p
+        else:
+            member = p * replicas + lax.rem(replica + side, replicas)
+        return pl.ds(pl.multiple_of(member * own + k * half, 16), half)
 
     wide = pl.ds(pl.multiple_of(tensor * (replicas * own), 16), replicas * own)
     ld_pool = load(pool_hbm, pool.at[replica])
@@ -87,8 +95,9 @@
     ld_down = load(down_hbm, down)
     near = []
     if square:
-        for i, member in enumerate((far, along, across, me)):
-            near.append(load(up_hbm.at[slab_of(member)], up_near.at[pl.ds(i * own, own)]))
+        order = [term(k, p, side) for side in (1, 0) for k, p in near_order[side]]
+        for i, rows in enumerate(order):
+            near.append(load(up_hbm.at[rows], up_near.at[pl.ds(i * half, half)]))
     ld_loss = load(loss_hbm, loss_src)
     ld_loss_own = load(loss_hbm.at[:, replica], loss_t.at[replica])
     ld_proj = load(proj_hbm, proj)
@@ -254,52 +263,68 @@
         hidden[t, r] = (dot(down[...], upstream[t, r]) * slope[r]).astype(bf16)
         if square:
             part[t, r, 0] = dot(up_near[:own, :], hidden[t, r]).astype(bf16)
-            part_in[t, r] = [
-                send(part.at[t, r, 0, low], relay.at[t, r, 0], PART, part_sems.at[r, 0], across),
-                send(part.at[t, r, 0, high], relay.at[t, r, 1], PART, part_sems.at[r, 1], along),
-            ]
+            part_in[t, r] = put_terms(t, r, 0)
+
+    def put_terms(t, r, p):
+        return [
+            send(part.at[t, r, p, rows], relay.at[t, r, 0, k, p], PART, part_sems.at[r, 2 * p + k], to)
+            for k, (to, rows) in enumerate(((along, low), (across, high)))
+        ]
 
     def stage_parts(t, r):
         if square:
             near_terms = dot(up_near[own:, :], hidden[t, r])
-            part[t, r, 1, high] = near_terms[half:own].astype(bf16)
-            part[t, r, 2, low] = near_terms[own:own + half].astype(bf16)
-            part_in[t, r] += [
-                send(part.at[t, r, 1, high], got.at[t, r, 0, high], PART, part_sems.at[r, 2], along),
-                send(part.at[t, r, 2, low], got.at[t, r, 1, low], PART, part_sems.at[r, 3], across),
-            ]
-            keep_part[r, 0] = near_terms[:half]
-            keep_part[r, 1] = near_terms[own + half:2 * own]
-            own_term = near_terms[2 * own:]
-        else:
-            part_in[t, r] = []
-            for by in range(1, members):
-                to = member_at(by)
-                part[t, r, by - 1] = dot(up[slab_of(to), :], hidden[t, r]).astype(bf16)
-                part_in[t, r].append(send(part.at[t, r, by - 1], got.at[t, r, by - 1], PART,
-                                          part_sems.at[r, by - 1], to))
-            own_term = dot(up[slab, :], hidden[t, r])
-        own_part[r] = own_term + upstream[t, r, slab, :].astype(f32)
+            part[t, r, 1] = near_terms[:own].astype(bf16)
+            part_in[t, r] += put_terms(t, r, 1)
+            for k in range(2):
+                for p in range(2):
+                    start = own + (2 * k + p) * half
+                    keep_part[r, k, p] = near_terms[start:start + half]
+            return
+        part_in[t, r] = []
+        for by in range(1, members):
+            to = member_at(by)
+            part[t, r, by - 1] = dot(up[slab_of(to), :], hidden[t, r]).astype(bf16)
+            part_in[t, r].append(send(part.at[t, r, by - 1], got.at[t, r, by - 1], PART,
+                                      part_sems.at[r, by - 1], to))
+        own_part[r] = dot(up[slab, :], hidden[t, r]) + upstream[t, r, slab, :].astype(f32)
 
     def stage_relay(t, r):
         if square:
-            for k, (to, rows) in enumerate(((along, low), (across, high))):
-                part_in[t, r][k].wait_recv()
-                part[t, r, k + 1, rows] = (keep_part[r, k] + relay[t, r, k].astype(f32)).astype(bf16)
-                part_in[t, r].append(send(part.at[t, r, k + 1, rows], got.at[t, r, k, rows], PART,
-                                          part_sems.at[r, 4 + k], to))
+            for p in range(2):
+                for k, to in enumerate((across, along)):
+                    part_in[t, r][2 * p + k].wait_recv()
+                    total = keep_part[r, k, p] + relay[t, r, 0, k, p].astype(f32)
+                    relay[t, r, 1, k, p] = total.astype(bf16)
+                    part_in[t, r].append(send(relay.at[t, r, 1, k, p], relay.at[t, r, 2, k, p], PART,
+                                              part_sems.at[r, 4 + 2 * p + k], to))
 
     def stage_sum(t, r):
-        for copy in part_in[t, r][2 if square else 0:]:
+        if square:
+            grad_in[t, r] = []
+            for p in range(2):
+                for k, to in enumerate((along, across)):
+                    part_in[t, r][4 + 2 * p + k].wait_recv()
+                    rows = term(k, p, 0)
+                    total = relay[t, r, 1, k, p].astype(f32) + relay[t, r, 2, k, p].astype(f32)
+                    grads[t, r, rows, :] = (total + upstream[t, r, rows, :].astype(f32)).astype(bf16)
+                    mine = grads.at[t, r, rows]
+                    grad_in[t, r].append(send(mine, mine, GRAD, grad_sems.at[r, 2 * p + k], to))
+            return
+        for copy in part_in[t, r]:
             copy.wait_recv()
         total = own_part[r]
         for k in range(got.shape[2]):
             total = total + got[t, r, k].astype(f32)
         grads[t, r, slab, :] = total.astype(bf16)
-        grad_in[t, r] = Gather(halves_of(grads.at[t, r]), grads.at[t, r, slab], GRAD, grad_sems.at[r])
+        grad_in[t, r] = Gather(halves_of(grads.at[t, r]), grads.at[t, r, slab], GRAD, grad_sems.at[r]).copies
+
+    def have_grads(t, r):
+        for copy in grad_in[t, r]:
+            copy.wait_recv()
 
     def stage_project(t, r):
-        grad_in[t, r].finish()
+        have_grads(t, r)
         edge[t, r, 0] = dot(proj[0], grads[t, r]).astype(bf16)
         if t == last:
             return
@@ -357,8 +382,6 @@
     for t in range(ticks):
         for r in every:
             stage_hidden(t, r)
-            if r > 0:
-                stage_relay(t, r - 1)
             stage_parts(t, r)
         if t < last:
             if t == 0:
@@ -371,12 +394,12 @@
             ])
             for copy in loss_in[t]:
                 pl.when(is_top)(copy.start)
-        settle(t, 0)
-        stage_relay(t, replicas - 1)
+        for r in every:
+            stage_relay(t, r)
+            if r == 0:
+                settle(t, r)
         for r in every:
             stage_sum(t, r)
-            if r == 0:
-                grad_in[t, r].follow()
             if r + 1 < replicas:
                 settle(t, r + 1)
         if t == last:
@@ -385,11 +408,8 @@
         else:
             for r in every:
                 pick_slope(t + 1, r)
-        for r in every:
-            grad_in[t, r].forward()
-            if r + 1 < replicas:
-                grad_in[t, r + 1].follow()
-            if t == 0:
+        if t == 0:
+            for r in every:
                 pool_t[:, pl.ds(r * saved, saved)] = pool[r].T
         if t == 0:
             write(pool_t, pool_out)
@@ -421,7 +441,7 @@
         for by in range(1, replicas)
     ]
     for r in every:
-        grad_in[last, r].finish()
+        have_grads(last, r)
         for k in range(2):
             edge[last, r, k] = dot(proj[k], grads[last, r]).astype(bf16)
             for by in range(1, replicas):
@@ -435,10 +455,11 @@
         copy.wait()
     all_sent(POOL, pool.at[pl.ds(0, replicas - 1)])
     all_sent(IDS, ids.at[pl.ds(0, replicas - 1)])
-    all_sent(SEED, part.at[0])
-    all_sent(PART, part)
-    all_sent(GRAD, part)
-    all_sent(UP, part.at[pl.ds(0, last)])
+    others = pl.ds(0, (members - 1) * own)
+    all_sent(SEED, upstream.at[0, :, others])
+    all_sent(PART, upstream if square else part)
+    all_sent(GRAD, upstream.at[:, :, pl.ds(0, 2 * own)] if square else part)
+    all_sent(UP, upstream.at[pl.ds(0, last), :, others])
     all_sent(INPUTS, in_got.at[pl.ds(0, replicas - 1)])
     all_sent(OUT, edge.at[last, pl.ds(0, replicas - 1)])
     pl.when(section > 0)(lambda: all_sent(DOWN, edge_got.at[:, :, 0]))
@@ -545,7 +566,7 @@
     dma = pltpu.SemaphoreType.DMA
     square = tensors == 2 and replicas == 2 and own_p % 32 == 0
     flows = 6 if square else members - 1
-    terms = 2 if square else members - 1
+    terms = 8 if square else members - 1
     scratch = [
         pltpu.VMEM(proj.shape, bf16), pltpu.VMEM(up.shape, bf16), pltpu.VMEM(down.shape, bf16),
         pltpu.VMEM(loss.shape, bf16), pltpu.VMEM((replicas,) + crop_ids.shape[1:], jnp.int32),
@@ -555,10 +576,10 @@
         pltpu.VMEM((ticks, replicas, width_p, rows), bf16),
         pltpu.VMEM((ticks, replicas, width_p, rows), bf16),
         pltpu.VMEM((ticks, replicas, hidden, rows), bf16),
-        pltpu.VMEM((ticks, replicas, members - 1, own_p, rows), bf16),
-        pltpu.VMEM((ticks, replicas, 2, own_p // 2, rows), bf16),
-        pltpu.VMEM((ticks, replicas, terms, own_p, rows), bf16),
-        pltpu.VMEM((replicas, 2, own_p // 2, rows), f32),
+        pltpu.VMEM((ticks, replicas, 2 if square else members - 1, own_p, rows), bf16),
+        pltpu.VMEM((ticks, replicas, 3, 2, 2, own_p // 2, rows) if square else (16, 128), bf16),
+        pltpu.VMEM((16, 128) if square else (ticks, replicas, members - 1, own_p, rows), bf16),
+        pltpu.VMEM((replicas, 2, 2, own_p // 2, rows) if square else (8, 128), f32),
         pltpu.VMEM((replicas, own_p, rows), f32),
         pltpu.VMEM((replicas, hidden, saved), bf16), pltpu.VMEM((replicas, hidden, saved), bf16),
         pltpu.VMEM((replicas, hidden, rows), f32),
@@ -568,9 +589,9 @@
         pltpu.VMEM((replicas, saved, width_p), f32),
         pltpu.VMEM((replicas * saved, hidden), bf16), pltpu.VMEM((replicas * saved, width_p), bf16),
         pltpu.VMEM((replicas * saved, width_p), bf16),
-        dma((12,)), dma((6,)), dma((11,)), dma((max(4, replicas - 1),)), dma((4, replicas - 1)),
+        dma((16,)), dma((6,)), dma((11,)), dma((max(4, replicas - 1),)), dma((4, replicas - 1)),
         dma((replicas - 1,)), dma((ticks - 1, replicas - 1)), dma((flows,)),
-        dma((replicas, flows)), dma((replicas, flows)), dma((replicas, flows)),
+        dma((replicas, terms)), dma((replicas, 4 if square else flows)), dma((replicas, flows)),
         dma((ticks - 1, replicas, 2)), dma((replicas - 1, 2)),
         pltpu.VMEM(up.shape if square else (16, 128), bf16),
     ]

time: 119 us -> 119 us (level)
  no operation moved by 1% of the time
where the time goes in v3:
time: 119 us; the launch traced here: 118 us
  Pallas kernels  118 us (99%)
    pallas_call x1, Pallas kernels, body(): pl.pallas_call(functools.partial(ticks_kernel, sections, tensors, replica...  113 us
    pallas_call x1, Pallas kernels, body(): pl.pallas_call(functools.partial(tail_kernel, replicas), out_shape=(shape...  4.59 us

profile of v3, /device:TPU:12, one launch (start us, length us, event | category | flops | bytes accessed | tf_op | source)
XLA Modules:
  0.0 118.5 jit_solution(15790723822814710065)
XLA Ops:
  0.6 113.1 %ticks.1 = (bf16[2,2,352,128]{3,2,1,0:T(8,128)(2,1)}, bf16[1408,256]{1,0:T(8,128)(2,1)}, bf16[768,256]{1,0:T(8,128)(2,1)}, bf16[256,768]{1,0:T(8,128)(2,1)}, bf1...) custom-call(bf16[2,2,352,128]{3,2,1,0:T(8,128)(2,1)} %bitcast.28, ...), custom_call_target="tpu_custom_call" | custom-call | tf_op jit(solution)/shard_map/ticks/pallas_call | solution.py:598
  113.7 4.6 %tail.1 = (bf16[768,1408]{1,0:T(8,128)(2,1)}, bf16[1408,768]{1,0:T(8,128)(2,1)}, bf16[2,352,1408]{2,1,0:T(8,128)(2,1)}, bf16[2,2,352,128]{3,2,1,0:T(8,128)(2,1)}) custom-call(f32[1]{0:T(128)} %bitcast.keep_ref, bf16[768,256]{1,0:T(8,128)(2,1)} %get-tuple-element.15.act_hbm, bf16[256,1408]{1,0:T(8,128)(2,1)} %get-tuple-element.16.sum_up_hbm, ...), custom_call_target="tpu_custom_call" | custom-call | tf_op jit(solution)/shard_map/tail/pallas_call | solution.py:627

commit v4 on v3

--- a/solution.py
+++ b/solution.py
@@ -1,4 +1,5 @@
 import functools
+import math
 
 import jax
 import jax.numpy as jnp
@@ -34,12 +35,12 @@
 def ticks_kernel(
     sections, tensors, replicas, own, ticks,
     inputs_hbm, pool_hbm, ids_hbm, seed_hbm, loss_hbm, proj_hbm, up_hbm, down_hbm,
-    in_got, pool_out, act_out, hidden_out, grad_out, up_out, out,
+    in_got, down_grad, up_grad, proj_grad, out,
     proj, up, down, loss_src, ids, loss_t, pool, pool_t, act_t,
     upstream, grads, hidden, part, relay, got, keep_part, own_part, slope_hi, slope_lo, slope,
     edge, edge_got, acc_hidden, acc_grad, acc_up, sum_hidden, sum_grad, sum_up,
-    load_sem, out_sem, send_sems, pool_sems, inputs_sems, ids_sems, loss_sems, seed_sems,
-    part_sems, grad_sems, up_sems, edge_sems, outgoing_sems, up_near,
+    load_sem, out_sem, send_sems, pool_sems, inputs_sems, ids_sems, loss_sems,
+    part_sems, grad_sems, up_sems, edge_sems, outgoing_sems, up_near, inputs,
 ):
     members = tensors * replicas
     square = tensors == 2 and replicas == 2 and own % 32 == 0
@@ -51,6 +52,7 @@
     hidden_rows = down.shape[0]
     saved = pool.shape[1]
     last = ticks - 1
+    mid = sections // 2
     along = (1 - tensor) * replicas + replica
     across = tensor * replicas + (1 - replica)
 
@@ -93,11 +95,10 @@
     ld_ids = load(ids_hbm, ids.at[replica])
     ld_up = load(up_hbm, up)
     ld_down = load(down_hbm, down)
-    near = []
     if square:
         order = [term(k, p, side) for side in (1, 0) for k, p in near_order[side]]
         for i, rows in enumerate(order):
-            near.append(load(up_hbm.at[rows], up_near.at[pl.ds(i * half, half)]))
+            pltpu.make_async_copy(up_hbm.at[rows], up_near.at[pl.ds(i * half, half)], out_sem.at[0]).start()
     ld_loss = load(loss_hbm, loss_src)
     ld_loss_own = load(loss_hbm.at[:, replica], loss_t.at[replica])
     ld_proj = load(proj_hbm, proj)
@@ -112,7 +113,6 @@
         pl.semaphore_signal(barrier, 1, device_id=device(other, me), device_id_type=MESH)
     pl.semaphore_wait(barrier, members - 1 + 3)
 
-    written = []
     POOL, IDS, SEED, PART, GRAD, UP, INPUTS, DOWN, SKIP, LOSS, OUT = range(11)
 
     def remote(src, dst, kind, recv_sem, s, member):
@@ -135,10 +135,21 @@
     def all_sent(kind, ref):
         pltpu.make_async_copy(ref, ref, send_sems.at[kind]).wait()
 
-    def write(src, dst):
-        copy = pltpu.make_async_copy(src, dst, out_sem.at[len(written)])
-        copy.start()
-        written.append(copy)
+    def lanes(r):
+        return inputs.at[:, :, pl.ds(pl.multiple_of(r * saved, 128), saved)]
+
+    chunk = 128
+    down_steps = [(start, min(chunk, hidden_rows - start)) for start in range(0, hidden_rows, chunk)]
+    up_steps = [(start, min(chunk, up_grad.shape[0] - start)) for start in range(0, up_grad.shape[0], chunk)]
+
+    def fill(count):
+        for _ in range(count):
+            if down_steps:
+                start, size = down_steps.pop(0)
+                down_grad[pl.ds(start, size), :] = dot(act_t[pl.ds(start, size), :], sum_up[...]).astype(bf16)
+            elif up_steps:
+                start, size = up_steps.pop(0)
+                up_grad[pl.ds(start, size), :] = dot(pool_t[pl.ds(start, size), :], sum_hidden[...]).astype(bf16)
 
     class Gather:
         def __init__(self, at, whole, kind, sems):
@@ -194,7 +205,7 @@
     else:
         pool_in = over_replicas(lambda r: pool.at[replica], pool.at[replica], POOL, pool_sems)
     ld_seed.wait()
-    seed_in = Gather(seed_at, upstream.at[0, replica, wide], SEED, seed_sems)
+    seed_in = Gather(seed_at, upstream.at[0, replica, wide], SEED, up_sems.at[0])
     seed_in.follow()
     ld_ids.wait()
     ids_in = over_replicas(lambda r: ids.at[replica], ids.at[replica], IDS, ids_sems)
@@ -218,8 +229,18 @@
         if hidden_rows % step:
             pre_at(hidden_rows - hidden_rows % step, hidden_rows % step)
 
+    def picks(t, r):
+        row = ids[r, pl.ds(t, 1), :]
+        place_of = lax.broadcasted_iota(jnp.int32, (saved, row.shape[1]), 0)
+        return jnp.where(place_of == row, 1.0, 0.0).astype(bf16)
+
+    def pick_slope(t, r):
+        chosen = picks(t, r)
+        slope[r] = dot(slope_hi[r], chosen) + dot(slope_lo[r], chosen)
+
     ld_up.wait()
     pre_slopes(replica)
+    pick_slope(0, replica)
     if square:
         pool_over = []
         for p in range(pieces):
@@ -234,25 +255,14 @@
         for by in range(1, replicas):
             pool_in[by - 1].wait_recv()
             pre_slopes(lax.rem(replica + replicas - by, replicas))
-    write(act_t, act_out)
     for copy in ids_in:
         copy.wait_recv()
-
-    def picks(t, r):
-        row = ids[r, pl.ds(t, 1), :]
-        place_of = lax.broadcasted_iota(jnp.int32, (saved, row.shape[1]), 0)
-        return jnp.where(place_of == row, 1.0, 0.0).astype(bf16)
-
-    def pick_slope(t, r):
-        chosen = picks(t, r)
-        slope[r] = dot(slope_hi[r], chosen) + dot(slope_lo[r], chosen)
-
-    for r in range(replicas):
-        pick_slope(0, r)
+    for by in range(1, replicas):
+        pick_slope(0, lax.rem(replica + by, replicas))
 
     ld_down.wait()
-    for copy in near:
-        copy.wait()
+    if square:
+        pltpu.make_async_copy(up_hbm, up_near, out_sem.at[0]).wait()
     seed_in.finish()
 
     up_in, part_in, grad_in, edge_in = {}, {}, {}, {}
@@ -329,27 +339,33 @@
         if t == last:
             return
         down_copy = remote(edge.at[t, r, 0], edge_got.at[t, r, 0], DOWN, edge_sems.at[t, r, 0], below, me)
-        pl.when(section > 0)(down_copy.start)
+        pl.when((section > 0) & (section != mid))(down_copy.start)
         skip = remote(edge.at[t, r, 1], edge_got.at[t, r, 1], SKIP, edge_sems.at[t, r, 1], mirror, me)
 
-        @pl.when(section >= sections // 2)
+        @pl.when(section > mid)
         def _():
             edge[t, r, 1] = dot(proj[1], grads[t, r]).astype(bf16)
             skip.start()
 
+        @pl.when(section == mid)
+        def _():
+            second = dot(proj[1], grads[t, r]).astype(bf16)
+            edge[t, r, 0] = (edge[t, r, 0].astype(f32) + second.astype(f32)).astype(bf16)
+            down_copy.start()
+
         edge_in[t, r] = (down_copy, skip)
 
     def stage_next(t, r):
         down_copy, skip = edge_in[t, r]
 
-        @pl.when(section < sections // 2)
+        @pl.when(section < mid - 1)
         def _():
             down_copy.wait_recv()
             skip.wait_recv()
             summed = edge_got[t, r, 0].astype(f32) + edge_got[t, r, 1].astype(f32)
             upstream[t + 1, r, slab, :] = summed.astype(bf16)
 
-        @pl.when((section >= sections // 2) & (section < sections - 1))
+        @pl.when((section >= mid - 1) & (section < sections - 1))
         def _():
             down_copy.wait_recv()
             upstream[t + 1, r, slab, :] = edge_got[t, r, 0]
@@ -376,61 +392,22 @@
         add(t, r, acc_hidden, sum_hidden, dot_nt(chosen, hidden[t, r]))
         add(t, r, acc_up, sum_up, dot_nt(chosen, upstream[t, r]))
 
-    every = range(replicas)
-    loss_in, inputs_in = [], []
-    slices = [(k, rows) for k in range(2) for rows in (low, pl.ds(half, own - half))]
-    for t in range(ticks):
-        for r in every:
-            stage_hidden(t, r)
-            stage_parts(t, r)
-        if t < last:
-            if t == 0:
-                ld_loss.wait()
-                ld_loss_own.wait()
-            loss_in.append([
-                remote(loss_src.at[t, replica_at(by)], loss_t.at[replica, t], LOSS,
-                       loss_sems.at[t, by - 1], section, tensor * replicas + replica_at(by))
-                for by in range(1, replicas)
-            ])
-            for copy in loss_in[t]:
-                pl.when(is_top)(copy.start)
-        for r in every:
-            stage_relay(t, r)
-            if r == 0:
-                settle(t, r)
-        for r in every:
-            stage_sum(t, r)
-            if r + 1 < replicas:
-                settle(t, r + 1)
-        if t == last:
-            write(sum_hidden, hidden_out)
-            write(sum_up, up_out)
-        else:
-            for r in every:
-                pick_slope(t + 1, r)
+    def give_loss(t):
         if t == 0:
-            for r in every:
-                pool_t[:, pl.ds(r * saved, saved)] = pool[r].T
-        if t == 0:
-            write(pool_t, pool_out)
-            ld_proj.wait()
-        if t == last:
-            break
-        for i, (k, rows) in enumerate(slices):
-            if i * last // len(slices) == t:
-                inputs_in += over_replicas(lambda r: inputs_hbm.at[k, r, rows], in_got.at[replica, k, rows],
-                                           INPUTS, inputs_sems.at[i])
-        for r in every:
-            stage_project(t, r)
-        for r in every:
-            stage_next(t, r)
-            if r == 0:
-                up_in[t + 1, r].follow()
-        for r in every:
-            add(t, r, acc_grad, sum_grad, dot_nt(picks(t, r), grads[t, r]))
-            up_in[t + 1, r].forward()
-            if r + 1 < replicas:
-                up_in[t + 1, r + 1].follow()
+            ld_loss.wait()
+            ld_loss_own.wait()
+        loss_in.append([
+            remote(loss_src.at[t, replica_at(by)], loss_t.at[replica, t], LOSS,
+                   loss_sems.at[t, by - 1], section, tensor * replicas + replica_at(by))
+            for by in range(1, replicas)
+        ])
+        for copy in loss_in[t]:
+            pl.when(is_top)(copy.start)
+
+    def give_inputs(t):
+        if t in (0, last):
+            for copy in inputs_in:
+                pl.when(section < mid if t == 0 else section >= mid)(copy.start)
 
     outs = [
         [
@@ -440,19 +417,87 @@
         ]
         for by in range(1, replicas)
     ]
-    for r in every:
+
+    def stage_outgoing(r):
         have_grads(last, r)
         for k in range(2):
             edge[last, r, k] = dot(proj[k], grads[last, r]).astype(bf16)
             for by in range(1, replicas):
                 pl.when(replica_at(by) == r)(outs[by - 1][k].start)
         add(last, r, acc_grad, sum_grad, dot_nt(picks(last, r), grads[last, r]))
-    write(sum_grad, grad_out)
-    write(edge.at[last, replica], out.at[:, replica])
-    for copy in inputs_in + [copy for pair in outs for copy in pair]:
+
+    every = range(replicas)
+    end = replicas - 1
+    loss_in, gathered = [], []
+    inputs_in = [
+        remote(inputs_hbm.at[k, replica_at(by), rows], in_got.at[replica, k, rows], INPUTS,
+               inputs_sems.at[2 * k + h, by - 1], section, tensor * replicas + replica_at(by))
+        for by in range(1, replicas)
+        for k in range(2)
+        for h, rows in enumerate((low, pl.ds(half, own - half)))
+    ]
+    for t in range(ticks):
+        project = stage_project if t < last else lambda t, r: stage_outgoing(r)
+        for r in every:
+            stage_hidden(t, r)
+            stage_parts(t, r)
+        if t < last:
+            give_loss(t)
+        for r in every:
+            stage_relay(t, r)
+            if r == 0:
+                settle(t, r)
+        for r in every:
+            stage_sum(t, r)
+            if r < end:
+                settle(t, r + 1)
+        if t < last:
+            for r in every:
+                pick_slope(t + 1, r)
+        else:
+            fill(10)
+        if t == 0:
+            for r in every:
+                pool_t[:, pl.ds(r * saved, saved)] = pool[r].T
+            ld_proj.wait()
+        give_inputs(t)
+        for r in every:
+            project(t, r)
+            if t == last and r < end:
+                fill(2)
+        if t == last:
+            break
+        for r in every:
+            stage_next(t, r)
+            if r == 0:
+                up_in[t + 1, r].follow()
+        for r in every:
+            add(t, r, acc_grad, sum_grad, dot_nt(picks(t, r), grads[t, r]))
+            up_in[t + 1, r].forward()
+            if r < end:
+                up_in[t + 1, r + 1].follow()
+
+    for copy in inputs_in:
         copy.wait_recv()
-    for copy in written:
+    for by in range(replicas):
+        r = replica_at(by)
+        src = inputs_hbm.at[:, r] if by == 0 else in_got.at[r]
+        gathered.append(pltpu.make_async_copy(src, lanes(r), out_sem.at[1 + by]))
+        gathered[by].start()
+    place = pltpu.make_async_copy(edge.at[last, replica], out.at[:, replica], out_sem.at[0])
+    place.start()
+    fill(len(down_steps) + len(up_steps))
+    for copy in gathered:
         copy.wait()
+    keep = jnp.where(section < sections // 2, 0.0, 1.0).astype(f32)
+    for k in range(2):
+        for start, size in ((0, half), (half, own - half)):
+            total = dot(inputs[k, pl.ds(start, size), :], sum_grad[...])
+            proj_grad[k, pl.ds(start, size), :] = (total * keep if k else total).astype(bf16)
+    place.wait()
+    for pair in outs:
+        for copy in pair:
+            copy.wait_recv()
     all_sent(POOL, pool.at[pl.ds(0, replicas - 1)])
     all_sent(IDS, ids.at[pl.ds(0, replicas - 1)])
     others = pl.ds(0, (members - 1) * own)
@@ -463,66 +508,15 @@
     all_sent(INPUTS, in_got.at[pl.ds(0, replicas - 1)])
     all_sent(OUT, edge.at[last, pl.ds(0, replicas - 1)])
     pl.when(section > 0)(lambda: all_sent(DOWN, edge_got.at[:, :, 0]))
-    pl.when(section >= sections // 2)(lambda: all_sent(SKIP, edge_got.at[:, :, 1]))
+    pl.when(section > mid)(lambda: all_sent(SKIP, edge_got.at[:, :, 1]))
     pl.when(is_top)(lambda: all_sent(LOSS, loss_t.at[pl.ds(0, replicas - 1)]))
 
 
-def tail_kernel(
-    replicas, keep_ref, act_hbm, sum_up_hbm, pool_hbm, sum_hidden_hbm, inputs_hbm, in_got_hbm,
-    sum_grad_hbm, outgoing_hbm,
-    down_out, up_out, proj_out, outgoing_out,
-    act, sum_up, pool, sum_hidden, inputs, sum_grad, outgoing, down_v, up_v, proj_v, load_sems, sems,
-):
-    replica = lax.axis_index("replica")
-    saved = sum_up.shape[0] // replicas
-    copies = []
-
-    def lanes(r):
-        return inputs.at[:, :, pl.ds(pl.multiple_of(r * saved, 128), saved)]
-
-    pairs = [
-        (act_hbm, act), (sum_up_hbm, sum_up), (pool_hbm, pool), (sum_hidden_hbm, sum_hidden),
-        (sum_grad_hbm, sum_grad), (outgoing_hbm, outgoing),
-        (inputs_hbm.at[:, replica], lanes(replica)),
-    ]
-    for by in range(1, replicas):
-        r = lax.rem(replica + by, replicas)
-        pairs.append((in_got_hbm.at[r], lanes(r)))
-    loads = [
-        pltpu.make_async_copy(src, dst, load_sems.at[i]) for i, (src, dst) in enumerate(pairs)
-    ]
-    for copy in loads:
+def tail_kernel(*refs):
+    pairs, sems = list(zip(refs[:4], refs[4:8])), refs[8]
+    copies = [pltpu.make_async_copy(src, dst, sems.at[i]) for i, (src, dst) in enumerate(pairs)]
+    for copy in copies:
         copy.start()
-
-    def put(src, dst):
-        copy = pltpu.make_async_copy(src, dst, sems.at[len(copies)])
-        copy.start()
-        copies.append(copy)
-
-    def finish(a, b, rows, kept, out, scale=None):
-        total = dot(a[rows], b[...])
-        if scale is not None:
-            total = total * scale
-        kept.at[rows][...] = total.astype(bf16)
-        put(kept.at[rows], out.at[rows])
-
-    loads[0].wait()
-    loads[1].wait()
-    for start in range(0, down_v.shape[0], 128):
-        finish(act, sum_up, pl.ds(start, min(128, down_v.shape[0] - start)), down_v, down_out)
-    loads[2].wait()
-    loads[3].wait()
-    for start in range(0, up_v.shape[0], 128):
-        finish(pool, sum_hidden, pl.ds(start, min(128, up_v.shape[0] - start)), up_v, up_out)
-    loads[5].wait()
-    put(outgoing, outgoing_out)
-    loads[4].wait()
-    for copy in loads[6:]:
-        copy.wait()
-    half = proj_v.shape[1] // 2
-    for k in range(2):
-        for start in (0, half):
-            finish(inputs, sum_grad, (k, pl.ds(start, half)), proj_v, proj_out, keep_ref[0] if k else None)
     for copy in copies:
         copy.wait()
 
@@ -531,7 +525,6 @@
     sections = lax.axis_size("section")
     tensors, replicas = lax.axis_size("tensor"), lax.axis_size("replica")
     members = tensors * replicas
-    encoder = lax.axis_index("section") < sections // 2
     own = w_proj.shape[2]
     own_p = -(-own // 16) * 16
     rows, width = incoming.shape[1], w_up.shape[1]
@@ -553,7 +546,6 @@
     proj = padded(padded(w_proj[0], 1), 2)
     up, down = padded(w_up[0], 0), padded(w_down[0], 1)
     pool_own = padded(pool_mixed[0], 1)
-    keep = jnp.where(encoder, 0.0, 1.0).astype(f32)[None]
     features = pool_inputs[0].transpose(1, 2, 0).reshape(2, replicas, own, saved)
     features = padded(features, 2)
     seed = padded(incoming[0].T, 0)
@@ -589,28 +581,27 @@
         pltpu.VMEM((replicas, saved, width_p), f32),
         pltpu.VMEM((replicas * saved, hidden), bf16), pltpu.VMEM((replicas * saved, width_p), bf16),
         pltpu.VMEM((replicas * saved, width_p), bf16),
-        dma((16,)), dma((6,)), dma((11,)), dma((max(4, replicas - 1),)), dma((4, replicas - 1)),
-        dma((replicas - 1,)), dma((ticks - 1, replicas - 1)), dma((flows,)),
+        dma((8,)), dma((1 + replicas,)), dma((11,)), dma((max(4, replicas - 1),)), dma((4, replicas - 1)),
+        dma((replicas - 1,)), dma((ticks - 1, replicas - 1)),
         dma((replicas, terms)), dma((replicas, 4 if square else flows)), dma((replicas, flows)),
         dma((ticks - 1, replicas, 2)), dma((replicas - 1, 2)),
         pltpu.VMEM(up.shape if square else (16, 128), bf16),
+        pltpu.VMEM((2, own_p, replicas * saved), bf16),
     ]
-    in_got, pool_t, act_t, sum_hidden, sum_grad, sum_up, out = pl.pallas_call(
+
+    kept_shapes = ((hidden, width_p), (width_p, hidden), (2, own_p, width_p), (2, replicas, own_p, rows))
+    vmem_limit = 66_800_000 - sum(2 * math.prod(dims) for dims in kept_shapes)
+    _, *kept = pl.pallas_call(
         functools.partial(ticks_kernel, sections, tensors, replicas, own_p, ticks),
         out_shape=(
             shape((replicas, 2, own_p, saved), bf16),
-            shape((width_p, replicas * saved), bf16),
-            shape((hidden, replicas * saved), bf16),
-            shape((replicas * saved, hidden), bf16),
-            shape((replicas * saved, width_p), bf16),
-            shape((replicas * saved, width_p), bf16),
-            shape((2, replicas, own_p, rows), bf16),
+            *(pltpu.VMEM(dims, bf16) for dims in kept_shapes),
         ),
         in_specs=[hbm] * 8,
-        out_specs=(hbm,) * 7,
+        out_specs=(hbm,) + (vmem,) * 4,
         scratch_shapes=scratch,
         compiler_params=pltpu.CompilerParams(
-            collective_id=0, has_side_effects=True, vmem_limit_bytes=60 * 1024 * 1024
+            collective_id=0, has_side_effects=True, vmem_limit_bytes=vmem_limit
         ),
         name="ticks",
     )(features, pool_own, crop_ids[0], seed, loss, proj, up, down)
@@ -623,26 +614,15 @@
         x = lax.slice_in_dim(x, 0, own, axis=axis + 1)
         return x.reshape(x.shape[:axis] + (count * own,) + x.shape[axis + 2:])
 
-    kept = (act_t, sum_up, pool_t, sum_hidden)
     grad_down, grad_up, grad_proj, outgoing = pl.pallas_call(
-        functools.partial(tail_kernel, replicas),
-        out_shape=(
-            shape((hidden, width_p), bf16), shape((width_p, hidden), bf16),
-            shape((2, own_p, width_p), bf16), shape(out.shape, bf16),
-        ),
-        in_specs=[pl.BlockSpec(memory_space=pltpu.SMEM)] + [hbm] * 8,
+        tail_kernel,
+        out_shape=tuple(shape(dims, bf16) for dims in kept_shapes),
+        in_specs=[vmem] * 4,
         out_specs=(hbm,) * 4,
-        scratch_shapes=[pltpu.VMEM(x.shape, bf16) for x in kept] + [
-            pltpu.VMEM((2, own_p, replicas * saved), bf16), pltpu.VMEM(sum_grad.shape, bf16),
-            pltpu.VMEM(out.shape, bf16),
-            pltpu.VMEM((hidden, width_p), bf16), pltpu.VMEM((width_p, hidden), bf16),
-            pltpu.VMEM((2, own_p, width_p), bf16),
-            dma((6 + replicas,)),
-            dma((-(-hidden // 128) - (-width_p // 128) + 5,)),
-        ],
-        compiler_params=pltpu.CompilerParams(vmem_limit_bytes=60 * 1024 * 1024),
+        scratch_shapes=[dma((4,))],
+        compiler_params=pltpu.CompilerParams(vmem_limit_bytes=128 * 1024),
         name="tail",
-    )(keep, *kept, features, in_got, sum_grad, out)
+    )(*kept)
     grad_down = trimmed(grad_down, 1)[None]
     grad_up = trimmed(grad_up, 0)[None]
     grad_proj = trimmed(trimmed(grad_proj, 1), 2)[None]

time: 119 us -> 115 us (0.966)
  Pallas kernels: 118 us -> 114 us
    pallas_call x1, Pallas kernels: 113 us -> 111 us  [body(): pl.pallas_call(functools.partial(ticks_kernel, sections, tensors, replica...]
    pallas_call x1, Pallas kernels: 4.59 us -> 2.79 us  [body(): pl.pallas_call(tail_kernel, out_shape=tuple((shape(dims, bf16) for dims i...]
where the time goes in v4:
time: 115 us
  Pallas kernels  114 us (99%)
    pallas_call x1, Pallas kernels, body(): pl.pallas_call(functools.partial(ticks_kernel, sections, tensors, replica...  111 us
    pallas_call x1, Pallas kernels, body(): pl.pallas_call(tail_kernel, out_shape=tuple((shape(dims, bf16) for dims i...  2.79 us

profile of v4, /device:TPU:12, one launch (start us, length us, event | category | flops | bytes accessed | tf_op | source)
XLA Modules:
  0.0 114.6 jit_solution(4703059863168963923)
XLA Ops:
  0.6 110.9 %ticks.1 = (bf16[2,2,352,128]{3,2,1,0:T(8,128)(2,1)}, bf16[768,1408]{1,0:T(8,128)(2,1)S(1)}, bf16[1408,768]{1,0:T(8,128)(2,1)S(1)}, bf16[2,352,1408]{2,1,0:T(8,128)(2,1)S(1)}, bf16[2,2,352,128]{3,2,1,0:T(8,128)(2,1)S(1)}) custom-call(bf16[2,2,352,128]{3,2,1,0:T(8,128)(2,1)} %bitcast.28, bf16[128,1408]{1,0:T(8,128)(2,1)} %bitcast.29, s32[4,128]{1,0:T(4,128)} %bitcast.31, ...), custom_call_target="tpu_custom_call" | custom-call | tf_op jit(solution)/shard_map/ticks/pallas_call | solution.py:594
  111.6 2.8 %tail.1 = (bf16[768,1408]{1,0:T(8,128)(2,1)}, bf16[1408,768]{1,0:T(8,128)(2,1)}, bf16[2,352,1408]{2,1,0:T(8,128)(2,1)}, bf16[2,2,352,128]{3,2,1,0:T(8,128)(2,1)}) custom-call(bf16[768,1408]{1,0:T(8,128)(2,1)S(1)} %get-tuple-element.12.refs_0_, bf16[1408,768]{1,0:T(8,128)(2,1)S(1)} %get-tuple-element.13.refs_1_, ...), custom_call_target="tpu_custom_call" | custom-call | tf_op jit(solution)/shard_map/tail/pallas_call | solution.py:617

commit v5 on v4

--- a/solution.py
+++ b/solution.py
@@ -153,29 +153,33 @@
 
     class Gather:
         def __init__(self, at, whole, kind, sems):
-            self.at, self.kind, self.sems = at, kind, sems
             if square:
-                self.copies = [self.put(me, 0, 0, along), self.put(me, 1, 1, across)]
+                flows = ((me, 0, along), (me, 1, across), (me, 1, along), (me, 0, across),
+                         (along, 0, across), (across, 1, along))
+                self.copies = [
+                    remote(at(member, h), at(member, h), kind, sems.at[i], section, to)
+                    for i, (member, h, to) in enumerate(flows)
+                ]
             else:
                 self.copies = [
-                    send(whole, whole, kind, sems.at[by - 1], member_at(by))
+                    remote(whole, whole, kind, sems.at[by - 1], section, member_at(by))
                     for by in range(1, members)
                 ]
 
-        def put(self, member, h, i, to):
-            ref = self.at(member, h)
-            return send(ref, ref, self.kind, self.sems.at[i], to)
+        def lead(self):
+            for copy in self.copies[:2 if square else None]:
+                copy.start()
 
         def follow(self):
             if square:
-                self.copies += [self.put(me, 1, 2, along), self.put(me, 0, 3, across)]
+                self.copies[2].start()
+                self.copies[3].start()
 
         def forward(self):
             if square:
-                self.copies[0].wait_recv()
-                self.copies.append(self.put(along, 0, 4, across))
-                self.copies[1].wait_recv()
-                self.copies.append(self.put(across, 1, 5, along))
+                for i in range(2):
+                    self.copies[i].wait_recv()
+                    self.copies[4 + i].start()
 
         def finish(self):
             for copy in self.copies[2 if square else 0:]:
@@ -206,6 +210,7 @@
         pool_in = over_replicas(lambda r: pool.at[replica], pool.at[replica], POOL, pool_sems)
     ld_seed.wait()
     seed_in = Gather(seed_at, upstream.at[0, replica, wide], SEED, up_sems.at[0])
+    seed_in.lead()
     seed_in.follow()
     ld_ids.wait()
     ids_in = over_replicas(lambda r: ids.at[replica], ids.at[replica], IDS, ids_sems)
@@ -327,7 +332,9 @@
         for k in range(got.shape[2]):
             total = total + got[t, r, k].astype(f32)
         grads[t, r, slab, :] = total.astype(bf16)
-        grad_in[t, r] = Gather(halves_of(grads.at[t, r]), grads.at[t, r, slab], GRAD, grad_sems.at[r]).copies
+        gather = Gather(halves_of(grads.at[t, r]), grads.at[t, r, slab], GRAD, grad_sems.at[r])
+        gather.lead()
+        grad_in[t, r] = gather.copies
 
     def have_grads(t, r):
         for copy in grad_in[t, r]:
@@ -338,10 +345,8 @@
         edge[t, r, 0] = dot(proj[0], grads[t, r]).astype(bf16)
         if t == last:
             return
-        down_copy = remote(edge.at[t, r, 0], edge_got.at[t, r, 0], DOWN, edge_sems.at[t, r, 0], below, me)
+        down_copy, skip = edge_in[t, r]
         pl.when((section > 0) & (section != mid))(down_copy.start)
-        skip = remote(edge.at[t, r, 1], edge_got.at[t, r, 1], SKIP, edge_sems.at[t, r, 1], mirror, me)
-
         @pl.when(section > mid)
         def _():
             edge[t, r, 1] = dot(proj[1], grads[t, r]).astype(bf16)
@@ -353,21 +358,11 @@
             edge[t, r, 0] = (edge[t, r, 0].astype(f32) + second.astype(f32)).astype(bf16)
             down_copy.start()
 
-        edge_in[t, r] = (down_copy, skip)
-
-    def stage_next(t, r):
-        down_copy, skip = edge_in[t, r]
-
-        @pl.when(section < mid - 1)
-        def _():
-            down_copy.wait_recv()
-            skip.wait_recv()
-            summed = edge_got[t, r, 0].astype(f32) + edge_got[t, r, 1].astype(f32)
-            upstream[t + 1, r, slab, :] = summed.astype(bf16)
-
+
+    def from_above(t, r):
         @pl.when((section >= mid - 1) & (section < sections - 1))
         def _():
-            down_copy.wait_recv()
+            edge_in[t, r][0].wait_recv()
             upstream[t + 1, r, slab, :] = edge_got[t, r, 0]
 
         @pl.when(is_top)
@@ -377,7 +372,16 @@
                     copy.wait_recv()
             upstream[t + 1, r, slab, :] = loss_t[r, t]
 
-        up_in[t + 1, r] = Gather(halves_of(upstream.at[t + 1, r]), upstream.at[t + 1, r, slab], UP, up_sems.at[r])
+    def stage_next(t, r):
+        @pl.when(section < mid - 1)
+        def _():
+            for copy in edge_in[t, r]:
+                copy.wait_recv()
+            summed = edge_got[t, r, 0].astype(f32) + edge_got[t, r, 1].astype(f32)
+            upstream[t + 1, r, slab, :] = summed.astype(bf16)
+
+        from_above(t, r)
+        up_in[t + 1, r].lead()
 
     def add(t, r, acc, total, term):
         rows = pl.ds(r * saved, saved)
@@ -426,9 +430,20 @@
                 pl.when(replica_at(by) == r)(outs[by - 1][k].start)
         add(last, r, acc_grad, sum_grad, dot_nt(picks(last, r), grads[last, r]))
 
+    def early(t):
+        return section >= sections - 1 - t
+
+    for t in range(last):
+        for r in range(replicas):
+            edge_in[t, r] = (
+                remote(edge.at[t, r, 0], edge_got.at[t, r, 0], DOWN, edge_sems.at[t, r, 0], below, me),
+                remote(edge.at[t, r, 1], edge_got.at[t, r, 1], SKIP, edge_sems.at[t, r, 1], mirror, me),
+            )
+            up_in[t + 1, r] = Gather(halves_of(upstream.at[t + 1, r]), upstream.at[t + 1, r, slab], UP, up_sems.at[r])
+
     every = range(replicas)
     end = replicas - 1
-    loss_in, gathered = [], []
+    loss_in = []
     inputs_in = [
         remote(inputs_hbm.at[k, replica_at(by), rows], in_got.at[replica, k, rows], INPUTS,
                inputs_sems.at[2 * k + h, by - 1], section, tensor * replicas + replica_at(by))
@@ -436,6 +451,19 @@
         for k in range(2)
         for h, rows in enumerate((low, pl.ds(half, own - half)))
     ]
+    gathered = [
+        pltpu.make_async_copy(
+            inputs_hbm.at[:, replica] if by == 0 else in_got.at[replica_at(by)], lanes(replica_at(by)), out_sem.at[1 + by]
+        )
+        for by in range(replicas)
+    ]
+
+    def take_inputs():
+        for copy in inputs_in:
+            copy.wait_recv()
+        for copy in gathered:
+            copy.start()
+
     for t in range(ticks):
         project = stage_project if t < last else lambda t, r: stage_outgoing(r)
         for r in every:
@@ -447,43 +475,57 @@
             stage_relay(t, r)
             if r == 0:
                 settle(t, r)
+            if t == last and r == 0:
+                for other in range(1, replicas):
+                    settle(t, other)
         for r in every:
             stage_sum(t, r)
             if r < end:
-                settle(t, r + 1)
+                fill(4) if t == last else settle(t, r + 1)
         if t < last:
+            @pl.when(early(t))
+            def _():
+                for r in every:
+                    from_above(t, r)
+                    up_in[t + 1, r].lead()
+                    up_in[t + 1, r].follow()
+
             for r in every:
                 pick_slope(t + 1, r)
         else:
-            fill(10)
+            fill(8)
         if t == 0:
             for r in every:
                 pool_t[:, pl.ds(r * saved, saved)] = pool[r].T
             ld_proj.wait()
         give_inputs(t)
+        if t == last:
+            pl.when(section < mid)(take_inputs)
         for r in every:
             project(t, r)
             if t == last and r < end:
                 fill(2)
         if t == last:
             break
-        for r in every:
-            stage_next(t, r)
-            if r == 0:
-                up_in[t + 1, r].follow()
+        pl.when(early(t))(lambda: [up_in[t + 1, r].forward() for r in every] and None)
+
+        @pl.when(jnp.logical_not(early(t)))
+        def _():
+            for r in every:
+                stage_next(t, r)
+                if r == 0:
+                    up_in[t + 1, r].follow()
+
         for r in every:
             add(t, r, acc_grad, sum_grad, dot_nt(picks(t, r), grads[t, r]))
-            up_in[t + 1, r].forward()
-            if r < end:
-                up_in[t + 1, r + 1].follow()
-
-    for copy in inputs_in:
-        copy.wait_recv()
-    for by in range(replicas):
-        r = replica_at(by)
-        src = inputs_hbm.at[:, r] if by == 0 else in_got.at[r]
-        gathered.append(pltpu.make_async_copy(src, lanes(r), out_sem.at[1 + by]))
-        gathered[by].start()
+
+            @pl.when(jnp.logical_not(early(t)))
+            def _():
+                up_in[t + 1, r].forward()
+                if r < end:
+                    up_in[t + 1, r + 1].follow()
+
+    pl.when(section >= mid)(take_inputs)
     place = pltpu.make_async_copy(edge.at[last, replica], out.at[:, replica], out_sem.at[0])
     place.start()
     fill(len(down_steps) + len(up_steps))

time: 115 us -> 114 us (level)
  Pallas kernels: 114 us -> 112 us
    pallas_call x1, Pallas kernels: 111 us -> 109 us  [body(): pl.pallas_call(functools.partial(ticks_kernel, sections, tensors, replica...]
where the time goes in v5:
time: 114 us; the launch traced here: 113 us
  Pallas kernels  112 us (98%)
    pallas_call x1, Pallas kernels, body(): pl.pallas_call(functools.partial(ticks_kernel, sections, tensors, replica...  109 us
    pallas_call x1, Pallas kernels, body(): pl.pallas_call(tail_kernel, out_shape=tuple((shape(dims, bf16) for dims i...  2.79 us

profile of v5, /device:TPU:12, one launch (start us, length us, event | category | flops | bytes accessed | tf_op | source)
XLA Modules:
  0.0 112.7 jit_solution(17476344584602936742)
XLA Ops:
  0.6 109.1 %ticks.1 = (bf16[2,2,352,128]{3,2,1,0:T(8,128)(2,1)}, bf16[768,1408]{1,0:T(8,128)(2,1)S(1)}, bf16[1408,768]{1,0:T(8,128)(2,1)S(1)}, bf16[2,352,1408]{2,1,0:T(8,128)(2,1)S(1)}, bf16[2,2,352,128]{3,2,1,0:T(8,128)(2,1)S(1)}) custom-call(bf16[2,2,352,128]{3,2,1,0:T(8,128)(2,1)} %bitcast.28, bf16[128,1408]{1,0:T(8,128)(2,1)} %bitcast.29, s32[4,128]{1,0:T(4,128)} %bitcast.31, ...), custom_call_target="tpu_custom_call" | custom-call | tf_op jit(solution)/shard_map/ticks/pallas_call | solution.py:636
  109.8 2.8 %tail.1 = (bf16[768,1408]{1,0:T(8,128)(2,1)}, bf16[1408,768]{1,0:T(8,128)(2,1)}, bf16[2,352,1408]{2,1,0:T(8,128)(2,1)}, bf16[2,2,352,128]{3,2,1,0:T(8,128)(2,1)}) custom-call(bf16[768,1408]{1,0:T(8,128)(2,1)S(1)} %get-tuple-element.12.refs_0_, bf16[1408,768]{1,0:T(8,128)(2,1)S(1)} %get-tuple-element.13.refs_1_, ...), custom_call_target="tpu_custom_call" | custom-call | tf_op jit(solution)/shard_map/tail/pallas_call | solution.py:659

commit v6 on v5

--- a/solution.py
+++ b/solution.py
@@ -342,16 +342,15 @@
 
     def stage_project(t, r):
         have_grads(t, r)
-        edge[t, r, 0] = dot(proj[0], grads[t, r]).astype(bf16)
-        if t == last:
-            return
         down_copy, skip = edge_in[t, r]
-        pl.when((section > 0) & (section != mid))(down_copy.start)
+
         @pl.when(section > mid)
         def _():
             edge[t, r, 1] = dot(proj[1], grads[t, r]).astype(bf16)
             skip.start()
 
+        edge[t, r, 0] = dot(proj[0], grads[t, r]).astype(bf16)
+        pl.when((section > 0) & (section != mid))(down_copy.start)
         @pl.when(section == mid)
         def _():
             second = dot(proj[1], grads[t, r]).astype(bf16)

time: 114 us -> 114 us (level)
  no operation moved by 1% of the time
where the time goes in v6:
time: 114 us; the launch traced here: 113 us
  Pallas kernels  113 us (99%)
    pallas_call x1, Pallas kernels, body(): pl.pallas_call(functools.partial(ticks_kernel, sections, tensors, replica...  110 us
    pallas_call x1, Pallas kernels, body(): pl.pallas_call(tail_kernel, out_shape=tuple((shape(dims, bf16) for dims i...  2.79 us

profile of v6, /device:TPU:12, one launch (start us, length us, event | category | flops | bytes accessed | tf_op | source)
XLA Modules:
  0.0 113.4 jit_solution(11941590872162480368)
XLA Ops:
  0.6 109.8 %ticks.1 = (bf16[2,2,352,128]{3,2,1,0:T(8,128)(2,1)}, bf16[768,1408]{1,0:T(8,128)(2,1)S(1)}, bf16[1408,768]{1,0:T(8,128)(2,1)S(1)}, bf16[2,352,1408]{2,1,0:T(8,128)(2,1)S(1)}, bf16[2,2,352,128]{3,2,1,0:T(8,128)(2,1)S(1)}) custom-call(bf16[2,2,352,128]{3,2,1,0:T(8,128)(2,1)} %bitcast.28, bf16[128,1408]{1,0:T(8,128)(2,1)} %bitcast.29, s32[4,128]{1,0:T(4,128)} %bitcast.31, ...), custom_call_target="tpu_custom_call" | custom-call | tf_op jit(solution)/shard_map/ticks/pallas_call | solution.py:635
  110.4 2.8 %tail.1 = (bf16[768,1408]{1,0:T(8,128)(2,1)}, bf16[1408,768]{1,0:T(8,128)(2,1)}, bf16[2,352,1408]{2,1,0:T(8,128)(2,1)}, bf16[2,2,352,128]{3,2,1,0:T(8,128)(2,1)}) custom-call(bf16[768,1408]{1,0:T(8,128)(2,1)S(1)} %get-tuple-element.12.refs_0_, bf16[1408,768]{1,0:T(8,128)(2,1)S(1)} %get-tuple-element.13.refs_1_, ...), custom_call_target="tpu_custom_call" | custom-call | tf_op jit(solution)/shard_map/tail/pallas_call | solution.py:658

commit v7 on v6

--- a/solution.py
+++ b/solution.py
@@ -154,11 +154,13 @@
     class Gather:
         def __init__(self, at, whole, kind, sems):
             if square:
-                flows = ((me, 0, along), (me, 1, across), (me, 1, along), (me, 0, across),
-                         (along, 0, across), (across, 1, along))
+                flows = [(me, h, part, to) for part in range(2) for h, to in enumerate((along, across))]
+                flows += [(me, 1, None, along), (me, 0, None, across)]
+                flows += [(to, h, part, on) for part in range(2) for h, (to, on) in
+                          enumerate(((along, across), (across, along)))]
                 self.copies = [
-                    remote(at(member, h), at(member, h), kind, sems.at[i], section, to)
-                    for i, (member, h, to) in enumerate(flows)
+                    remote(at(member, h, part), at(member, h, part), kind, sems.at[i], section, to)
+                    for i, (member, h, part, to) in enumerate(flows)
                 ]
             else:
                 self.copies = [
@@ -167,30 +169,35 @@
                 ]
 
         def lead(self):
-            for copy in self.copies[:2 if square else None]:
+            for copy in self.copies[:4 if square else None]:
                 copy.start()
 
         def follow(self):
             if square:
-                self.copies[2].start()
-                self.copies[3].start()
+                self.copies[4].start()
+                self.copies[5].start()
 
         def forward(self):
             if square:
-                for i in range(2):
+                for i in range(4):
                     self.copies[i].wait_recv()
-                    self.copies[4 + i].start()
+                    self.copies[6 + i].start()
 
         def finish(self):
-            for copy in self.copies[2 if square else 0:]:
+            for copy in self.copies[4 if square else 0:]:
                 copy.wait_recv()
 
+    def part_rows(start, size, part):
+        cut = -(-size // 32) * 16
+        begin, count = {None: (0, size), 0: (0, cut), 1: (cut, size - cut)}[part]
+        return pl.ds(pl.multiple_of(start + begin, 16), count)
+
     def halves_of(ref):
-        return lambda member, h: ref.at[pl.ds(pl.multiple_of(member * own + h * half, 16), half)]
-
-    def seed_at(member, h):
-        return upstream.at[0, lax.rem(member, replicas),
-                           pl.ds(pl.multiple_of(lax.div(member, replicas) * (replicas * own) + h * own, 16), own)]
+        return lambda member, h, part: ref.at[part_rows(member * own + h * half, half, part)]
+
+    def seed_at(member, h, part):
+        start = lax.div(member, replicas) * (replicas * own) + h * own
+        return upstream.at[0, lax.rem(member, replicas), part_rows(start, own, part)]
 
     slab = slab_of(me)
     low, high = pl.ds(0, half), pl.ds(half, half)
@@ -414,9 +421,10 @@
 
     outs = [
         [
-            remote(edge.at[last, replica_at(by), k], out.at[k, replica], OUT,
-                   outgoing_sems.at[by - 1, k], section, tensor * replicas + replica_at(by))
+            remote(edge.at[last, replica_at(by), k, rows], out.at[k, replica, rows], OUT,
+                   outgoing_sems.at[by - 1, 2 * k + h], section, tensor * replicas + replica_at(by))
             for k in range(2)
+            for h, rows in enumerate((low, pl.ds(half, own - half)))
         ]
         for by in range(1, replicas)
     ]
@@ -424,10 +432,11 @@
     def stage_outgoing(r):
         have_grads(last, r)
         for k in range(2):
-            edge[last, r, k] = dot(proj[k], grads[last, r]).astype(bf16)
-            for by in range(1, replicas):
-                pl.when(replica_at(by) == r)(outs[by - 1][k].start)
-        add(last, r, acc_grad, sum_grad, dot_nt(picks(last, r), grads[last, r]))
+            for h, (start, size) in enumerate(((0, half), (half, own - half))):
+                rows = pl.ds(start, size)
+                edge[last, r, k, rows] = dot(proj[k, rows], grads[last, r]).astype(bf16)
+                for by in range(1, replicas):
+                    pl.when(replica_at(by) == r)(outs[by - 1][2 * k + h].start)
 
     def early(t):
         return section >= sections - 1 - t
@@ -502,8 +511,6 @@
             pl.when(section < mid)(take_inputs)
         for r in every:
             project(t, r)
-            if t == last and r < end:
-                fill(2)
         if t == last:
             break
         pl.when(early(t))(lambda: [up_in[t + 1, r].forward() for r in every] and None)
@@ -525,6 +532,8 @@
                     up_in[t + 1, r + 1].follow()
 
     pl.when(section >= mid)(take_inputs)
+    for r in every:
+        add(last, r, acc_grad, sum_grad, dot_nt(picks(last, r), grads[last, r]))
     place = pltpu.make_async_copy(edge.at[last, replica], out.at[:, replica], out_sem.at[0])
     place.start()
     fill(len(down_steps) + len(up_steps))
@@ -598,7 +607,7 @@
     hbm = pl.BlockSpec(memory_space=pl.ANY)
     dma = pltpu.SemaphoreType.DMA
     square = tensors == 2 and replicas == 2 and own_p % 32 == 0
-    flows = 6 if square else members - 1
+    flows = 10 if square else members - 1
     terms = 8 if square else members - 1
     scratch = [
         pltpu.VMEM(proj.shape, bf16), pltpu.VMEM(up.shape, bf16), pltpu.VMEM(down.shape, bf16),
@@ -625,7 +634,7 @@
         dma((8,)), dma((1 + replicas,)), dma((11,)), dma((max(4, replicas - 1),)), dma((4, replicas - 1)),
         dma((replicas - 1,)), dma((ticks - 1, replicas - 1)),
         dma((replicas, terms)), dma((replicas, 4 if square else flows)), dma((replicas, flows)),
-        dma((ticks - 1, replicas, 2)), dma((replicas - 1, 2)),
+        dma((ticks - 1, replicas, 2)), dma((replicas - 1, 4)),
         pltpu.VMEM(up.shape if square else (16, 128), bf16),
         pltpu.VMEM((2, own_p, replicas * saved), bf16),
     ]

time: 114 us -> 113 us (level)
  no operation moved by 1% of the time
where the time goes in v7:
time: 113 us
  Pallas kernels  112 us (99%)
    pallas_call x1, Pallas kernels, body(): pl.pallas_call(functools.partial(ticks_kernel, sections, tensors, replica...  109 us
    pallas_call x1, Pallas kernels, body(): pl.pallas_call(tail_kernel, out_shape=tuple((shape(dims, bf16) for dims i...  2.79 us

profile of v7, /device:TPU:12, one launch (start us, length us, event | category | flops | bytes accessed | tf_op | source)
XLA Modules:
  0.0 112.9 jit_solution(3424203573256548026)
XLA Ops:
  0.6 109.3 %ticks.1 = (bf16[2,2,352,128]{3,2,1,0:T(8,128)(2,1)}, bf16[768,1408]{1,0:T(8,128)(2,1)S(1)}, bf16[1408,768]{1,0:T(8,128)(2,1)S(1)}, bf16[2,352,1408]{2,1,0:T(8,128)(2,1)S(1)}, bf16[2,2,352,128]{3,2,1,0:T(8,128)(2,1)S(1)}) custom-call(bf16[2,2,352,128]{3,2,1,0:T(8,128)(2,1)} %bitcast.28, bf16[128,1408]{1,0:T(8,128)(2,1)} %bitcast.29, s32[4,128]{1,0:T(4,128)} %bitcast.31, ...), custom_call_target="tpu_custom_call" | custom-call | tf_op jit(solution)/shard_map/ticks/pallas_call | solution.py:644
  109.9 2.8 %tail.1 = (bf16[768,1408]{1,0:T(8,128)(2,1)}, bf16[1408,768]{1,0:T(8,128)(2,1)}, bf16[2,352,1408]{2,1,0:T(8,128)(2,1)}, bf16[2,2,352,128]{3,2,1,0:T(8,128)(2,1)}) custom-call(bf16[768,1408]{1,0:T(8,128)(2,1)S(1)} %get-tuple-element.12.refs_0_, bf16[1408,768]{1,0:T(8,128)(2,1)S(1)} %get-tuple-element.13.refs_1_, ...), custom_call_target="tpu_custom_call" | custom-call | tf_op jit(solution)/shard_map/tail/pallas_call | solution.py:667

commit v8 on v7

--- a/solution.py
+++ b/solution.py
@@ -223,7 +223,7 @@
     ids_in = over_replicas(lambda r: ids.at[replica], ids.at[replica], IDS, ids_sems)
     is_top = section == sections - 1
 
-    step = 256 if hidden_rows % 256 == 0 else 128
+    step = next(n for n in (384, 256, 128) if hidden_rows % n == 0 or n == 128)
 
     def pre_slopes(r):
         def pre_at(start, size):

time: 113 us -> 113 us (level)
  no operation moved by 1% of the time
where the time goes in v8:
time: 113 us
  Pallas kernels  112 us (99%)
    pallas_call x1, Pallas kernels, body(): pl.pallas_call(functools.partial(ticks_kernel, sections, tensors, replica...  109 us
    pallas_call x1, Pallas kernels, body(): pl.pallas_call(tail_kernel, out_shape=tuple((shape(dims, bf16) for dims i...  2.79 us

profile of v8, /device:TPU:12, one launch (start us, length us, event | category | flops | bytes accessed | tf_op | source)
XLA Modules:
  0.0 112.8 jit_solution(8935437612649671896)
XLA Ops:
  0.6 109.2 %ticks.1 = (bf16[2,2,352,128]{3,2,1,0:T(8,128)(2,1)}, bf16[768,1408]{1,0:T(8,128)(2,1)S(1)}, bf16[1408,768]{1,0:T(8,128)(2,1)S(1)}, bf16[2,352,1408]{2,1,0:T(8,128)(2,1)S(1)}, bf16[2,2,352,128]{3,2,1,0:T(8,128)(2,1)S(1)}) custom-call(bf16[2,2,352,128]{3,2,1,0:T(8,128)(2,1)} %bitcast.28, bf16[128,1408]{1,0:T(8,128)(2,1)} %bitcast.29, s32[4,128]{1,0:T(4,128)} %bitcast.31, ...), custom_call_target="tpu_custom_call" | custom-call | tf_op jit(solution)/shard_map/ticks/pallas_call | solution.py:644
  109.9 2.8 %tail.1 = (bf16[768,1408]{1,0:T(8,128)(2,1)}, bf16[1408,768]{1,0:T(8,128)(2,1)}, bf16[2,352,1408]{2,1,0:T(8,128)(2,1)}, bf16[2,2,352,128]{3,2,1,0:T(8,128)(2,1)}) custom-call(bf16[768,1408]{1,0:T(8,128)(2,1)S(1)} %get-tuple-element.12.refs_0_, bf16[1408,768]{1,0:T(8,128)(2,1)S(1)} %get-tuple-element.13.refs_1_, ...), custom_call_target="tpu_custom_call" | custom-call | tf_op jit(solution)/shard_map/tail/pallas_call | solution.py:667
